TPU v7x, 128 devices: a whole 4x4x4 slice. The times are simulated.
128 devices in a mesh: chan: 16 (over z, x_hi, core), win: 8 (over y, x_lo).
Axes of the slice: x: 4 (x_hi: 2, x_lo: 2; x = x_hi * 2 + x_lo), y: 4, z: 4, core: 2. Of those that a mesh axis runs over, the one named last changes fastest.
Arguments:
- series: bfloat16 [64, 2048, 1500], P('win', 'chan'), may hold values from -1700 to 1700
- validity: int32 [64, 2048], P('win', 'chan'), may hold values from 0 to 1, as said below
Outputs:
- source_gathers: float32 [2048, 16, 8, 16, 128], P('chan', None, 'win')
Inputs may be any that keep to these rules, and one draw needn't show every extreme that they name: `validity`: a channel flagged dead is 0 in every window.
All inputs are finite; a program needn't handle non-finite values.
Results may differ from a plain program's by a relative error of at most 0.0037.
Values may be sent and summed in bfloat16 or wider, within the bound.
No kernel may reach another device: no remote copies, remote signals or barrier semaphores. Data moves between devices by JAX's collectives and lax.ppermute only.
A program may use at most 192 MiB of HBM per device.

v0:
```python
import math

import jax
import jax.numpy as jnp
import numpy as np
from jax import lax
from jax.experimental import pallas as pl
from jax.experimental.pallas import tpu as pltpu
from jax.sharding import PartitionSpec as P

SAMPLES = 1500
BINS = 128
LAGS = 128
LOWEST = 6
ROWS = BINS + 1
CHUNK = 43
STEPS = ROWS // CHUNK
PITCH = 2 * BINS + 8
ROW = 24
SPAN = 512
VMEM_LIMIT = 60 << 20


def build_tables():
    t = np.arange(SAMPLES)
    k = np.arange(BINS) + LOWEST
    angle = ((t[:, None] * k[None, :]) % SAMPLES).astype(np.float32) * np.float32(2.0 * math.pi / SAMPLES)
    hann = np.float32(0.5) - np.float32(0.5) * np.cos(t.astype(np.float32) * np.float32(2.0 * math.pi / SAMPLES))
    taper = np.concatenate([hann[:, None] * np.cos(angle), -hann[:, None] * np.sin(angle)], axis=1)
    taper = np.pad(taper.T, ((0, 0), (0, -SAMPLES % SPAN))).astype(jnp.bfloat16)
    j = np.arange(LAGS) - LAGS // 2
    lag_angle = ((k[:, None] * j[None, :]) % SAMPLES).astype(np.float32) * np.float32(2.0 * math.pi / SAMPLES)
    inverse = np.concatenate([np.cos(lag_angle), -np.sin(lag_angle)], axis=0)
    inverse = np.ascontiguousarray(inverse.T).astype(np.float32)
    high = inverse.astype(jnp.bfloat16)
    low = (inverse - high.astype(np.float32)).astype(jnp.bfloat16)
    return taper, high, low


def spectra_call(series, validity, taper):
    windows, channels, _ = series.shape
    slots = channels // 16
    groups = BINS // 8 + 1
    steps = taper.shape[1] // SPAN
    tail = SAMPLES - (steps - 1) * SPAN
    by_time = jnp.transpose(series, (2, 0, 1))

    def kernel(x_ref, v_ref, t_ref, w_ref, p_ref, turned, acc, scr):
        g = pl.program_id(0)

        def turn(q, _):
            block = x_ref[pl.ds(q * 4, 4)].astype(jnp.float32)
            for e in range(4):
                turned[pl.ds(q * 4 + e, windows, stride=SPAN + 8), :] = block[e]
            return 0

        @pl.when(g == 0)
        def _():
            acc[...] = jnp.zeros_like(acc)

        @pl.when(g < steps - 1)
        def _():
            lax.fori_loop(0, SPAN // 4, turn, 0, unroll=16)

        @pl.when(g == steps - 1)
        def _():
            lax.fori_loop(0, tail // 4, turn, 0, unroll=17)
            for q in range(tail, SPAN):
                turned[pl.ds(q, windows, stride=SPAN + 8), :] = jnp.zeros((windows, channels), jnp.float32)

        for h in range(windows // 2):
            cols = [turned[(2 * h + e) * (SPAN + 8) : (2 * h + e) * (SPAN + 8) + SPAN, :] for e in range(2)]
            cols = jnp.concatenate(cols, axis=1).astype(jnp.bfloat16)
            acc[h] += jnp.dot(t_ref[...], cols, preferred_element_type=jnp.float32)

        @pl.when(g == steps - 1)
        def _():
            for h in range(windows // 2):
                s = acc[h]
                energy = jnp.sum(s * s, axis=0, keepdims=True) * (1.0 / (2 * BINS))
                flags = v_ref[2 * h : 2 * h + 2, :].astype(jnp.float32)
                flags = jnp.concatenate([flags[0:1], flags[1:2]], axis=1)
                s = s * lax.rsqrt(energy + 1e-06) * flags
                for e in range(2):
                    for part in range(2):
                        scr[pl.ds(part * 8 + 2 * h + e, BINS, stride=16), :] = s[
                            part * BINS : (part + 1) * BINS, e * channels : (e + 1) * channels
                        ]
            for b in range(BINS // 8):
                block = scr[b * 128 : (b + 1) * 128, :]
                w_ref[b * 8 : (b + 1) * 8] = block.astype(jnp.bfloat16).reshape(8, 16, channels)
                p_ref[:, b] = block.T.astype(jnp.bfloat16).reshape(slots, 16, 128)
            f = v_ref[...].astype(jnp.float32)
            f = jnp.concatenate([f, jnp.zeros((8, channels), jnp.float32)], axis=0)
            w_ref[BINS] = f.astype(jnp.bfloat16)
            f = jnp.concatenate([f, jnp.zeros((112, channels), jnp.float32)], axis=0)
            p_ref[:, groups - 1] = f.T.astype(jnp.bfloat16).reshape(slots, 16, 128)

    return pl.pallas_call(
        kernel,
        grid=(steps,),
        in_specs=[
            pl.BlockSpec((SPAN, windows, channels), lambda g: (g, 0, 0)),
            pl.BlockSpec((windows, channels), lambda g: (0, 0)),
            pl.BlockSpec((2 * BINS, SPAN), lambda g: (0, g)),
        ],
        out_specs=[
            pl.BlockSpec((ROWS, 16, channels), lambda g: (0, 0, 0)),
            pl.BlockSpec((slots, groups, 16, 128), lambda g: (0, 0, 0, 0)),
        ],
        out_shape=[
            jax.ShapeDtypeStruct((ROWS, 16, channels), jnp.bfloat16),
            jax.ShapeDtypeStruct((slots, groups, 16, 128), jnp.bfloat16),
        ],
        scratch_shapes=[
            pltpu.VMEM((windows * (SPAN + 8), channels), jnp.float32),
            pltpu.VMEM((windows // 2, 2 * BINS, 2 * channels), jnp.float32),
            pltpu.VMEM((BINS * 16, channels), jnp.float32),
        ],
        compiler_params=pltpu.CompilerParams(dimension_semantics=("arbitrary",), vmem_limit_bytes=VMEM_LIMIT),
        name="spectra",
    )(by_time, validity, taper)


def slot_call(order, parts):
    count, groups = parts.shape[:2]

    span = 6
    steps = pl.cdiv(groups, span)
    whole = groups - 1 - (steps - 1) * span

    def kernel(order_ref, p_ref, r_ref):
        g = pl.program_id(0)

        def body(b, _):
            tiles = [p_ref[order_ref[q], b] for q in range(count)]
            for e in range(8):
                r_ref[b * 8 + e] = jnp.concatenate([t[:, 16 * e : 16 * e + 16] for t in tiles], axis=1)
            return 0

        @pl.when(g < steps - 1)
        def _():
            lax.fori_loop(0, span, body, 0, unroll=span)

        @pl.when(g == steps - 1)
        def _():
            lax.fori_loop(0, whole, body, 0, unroll=whole)
            r_ref[whole * 8] = jnp.concatenate([p_ref[order_ref[q], whole][:, :16] for q in range(count)], axis=1)

    return pl.pallas_call(
        kernel,
        grid_spec=pltpu.PrefetchScalarGridSpec(
            num_scalar_prefetch=1,
            grid=(steps,),
            in_specs=[pl.BlockSpec((count, span, 16, 128), lambda g, o: (0, g, 0, 0))],
            out_specs=pl.BlockSpec((span * 8, 16, 128), lambda g, o: (g, 0, 0)),
        ),
        out_shape=jax.ShapeDtypeStruct((ROWS, 16, 128), jnp.bfloat16),
        compiler_params=pltpu.CompilerParams(dimension_semantics=("arbitrary",), vmem_limit_bytes=VMEM_LIMIT),
        name="slot",
    )(order, parts)


def pair_call(places, sources, receivers, high, low, blocks, previous=None):
    count = len(receivers)
    rows = 16 * count

    def kernel(place_ref, *refs):
        src = refs[:8]
        rcv = refs[8 : 8 + count]
        hi_ref, lo_ref = refs[8 + count : 10 + count]
        out, joined, recip, held, sent = refs[-5:]
        g = pl.program_id(0)

        def one_bin(k):
            tiles = [s[k] for s in src]
            swapped = []
            for tile in tiles:
                f = tile.astype(jnp.float32)
                swapped.append(jnp.concatenate([-f[8:], f[:8]], axis=0).astype(jnp.bfloat16))
            weights = jnp.concatenate([jnp.concatenate(tiles, axis=0), jnp.concatenate(swapped, axis=0)], axis=1)
            lhs = jnp.concatenate([r[k] for r in rcv], axis=0)
            return jnp.dot(lhs, weights, preferred_element_type=jnp.float32)

        def store_bin(k, _):
            both = one_bin(k)
            at = g * CHUNK + k
            joined[pl.ds(at, rows, stride=PITCH), :] = both[:, :128]
            joined[pl.ds(at + BINS, rows, stride=PITCH), :] = both[:, 128:]
            return 0

        @pl.when(g < STEPS)
        def _():
            lax.fori_loop(0, CHUNK - 1, store_bin, 0, unroll=42)

        @pl.when(g < STEPS - 1)
        def _():
            store_bin(CHUNK - 1, 0)

        @pl.when(g == STEPS - 1)
        def _():
            recip[...] = 1.0 / jnp.maximum(one_bin(CHUNK - 1)[:, :128], 1.0)

        @pl.when(g >= STEPS)
        def _():
            block = g - STEPS
            slot = lax.rem(block, 2)

            def write(which, at):
                return pltpu.make_async_copy(
                    held.at[at, :, pl.ds(0, 16), :], out.at[:, place_ref[which], 0], sent.at[at]
                )

            @pl.when(block >= 2)
            def _():
                write(block - 2, slot).wait()

            flat = held.at[slot].reshape(128 * ROW, LAGS)

            def body(q, _):
                i = (g - STEPS) * 16 + 2 * q
                first = pl.multiple_of(i * PITCH, 8)
                second = pl.multiple_of((i + 1) * PITCH, 8)
                pair = jnp.concatenate([joined[pl.ds(first, 256), :], joined[pl.ds(second, 256), :]], axis=1)
                upper = pair.astype(jnp.bfloat16)
                lower = (pair - upper.astype(jnp.float32)).astype(jnp.bfloat16)
                tables = jnp.concatenate([hi_ref[...], lo_ref[...]], axis=0)
                acc = jnp.dot(tables, upper, preferred_element_type=jnp.float32)
                acc = acc[:LAGS] + acc[LAGS:] + jnp.dot(hi_ref[...], lower, preferred_element_type=jnp.float32)
                scale = jnp.concatenate([recip[pl.ds(i, 1), :], recip[pl.ds(i + 1, 1), :]], axis=1)
                acc = acc * scale
                flat[pl.ds(2 * q, 128, stride=ROW), :] = acc[:, :128].T
                flat[pl.ds(2 * q + 1, 128, stride=ROW), :] = acc[:, 128:].T
                return 0

            lax.fori_loop(0, 8, body, 0, unroll=8)
            write(block, slot).start()

            @pl.when(block == count - 1)
            def _():
                write(block - 1, 1 - slot).wait()
                write(block, slot).wait()

    piece = pl.BlockSpec((CHUNK, 16, 128), lambda g, at: (jnp.minimum(g, STEPS - 1), 0, 0))
    table = pl.BlockSpec((LAGS, 2 * BINS), lambda g, at: (0, 0))
    in_specs = [piece] * (8 + count) + [table] * 2
    operands = [*sources, *receivers, high, low]
    aliases = {}
    if previous is not None:
        in_specs.append(pl.BlockSpec(memory_space=pl.ANY))
        aliases = {1 + len(operands): 0}
        operands.append(previous)
    macs = (ROWS * 128 * 256 + 128 * 128 * 256 * 3) * rows
    return pl.pallas_call(
        kernel,
        grid_spec=pltpu.PrefetchScalarGridSpec(
            num_scalar_prefetch=1,
            grid=(STEPS + count,),
            in_specs=in_specs,
            out_specs=pl.BlockSpec(memory_space=pl.ANY),
            scratch_shapes=[
                pltpu.VMEM((rows * PITCH, 128), jnp.float32),
                pltpu.VMEM((rows, 128), jnp.float32),
                pltpu.VMEM((2, 128, ROW, LAGS), jnp.float32),
                pltpu.SemaphoreType.DMA((2,)),
            ],
        ),
        out_shape=jax.ShapeDtypeStruct((128, blocks, 1, 16, LAGS), jnp.float32),
        input_output_aliases=aliases,
        compiler_params=pltpu.CompilerParams(dimension_semantics=("arbitrary",), vmem_limit_bytes=VMEM_LIMIT),
        cost_estimate=pl.CostEstimate(flops=2 * macs, bytes_accessed=(8 + count) * ROWS * 4096, transcendentals=0),
    )(places, *operands)


def solution(mesh):
    taper, high, low = build_tables()

    def chan_of(z, h, c):
        return (z % 4) * 4 + (h % 2) * 2 + c % 2

    def win_of(y, x):
        return (y % 4) * 2 + x % 2

    def over_chan(a, dz=0, dh=0, dc=0):
        perm = [(chan_of(z, h, c), chan_of(z + dz, h + dh, c + dc)) for z in range(4) for h in range(2) for c in range(2)]
        return lax.ppermute(a, "chan", perm)

    def over_win(a, dy=0, dx=0):
        perm = [(win_of(y, x), win_of(y + dy, x + dx)) for y in range(4) for x in range(2)]
        return lax.ppermute(a, "win", perm)

    ring_order = ((0, 0), (0, 1), (-1, 0), (1, 0), (-1, 1), (1, 1), (-2, 0), (2, 1))

    def step(move, value, **by):
        return move(value, **by)

    def stages(series, validity):
        own, slots = spectra_call(series, validity, taper)

        parts = lax.all_to_all(slots, "win", split_axis=0, concat_axis=0, tiled=True)
        side = step(over_win, own, dx=1)
        up, down = step(over_win, own, dy=1), step(over_win, own, dy=-1)
        side_up, side_down = step(over_win, side, dy=1), step(over_win, side, dy=-1)
        far, side_far = step(over_win, up, dy=1), step(over_win, side_down, dy=-1)
        sources = [own, side, up, down, side_up, side_down, far, side_far]

        w = lax.axis_index("win")
        y, x = w // 2, w % 2
        order = jnp.stack([((y + dy) % 4) * 2 + (x + dx) % 2 for dy, dx in ring_order]).astype(jnp.int32)
        mine = slot_call(order, parts)
        side = step(over_chan, mine, dh=1)
        up, down = step(over_chan, mine, dz=1), step(over_chan, mine, dz=-1)
        side_up, side_down = step(over_chan, side, dz=1), step(over_chan, side, dz=-1)
        far, side_far = step(over_chan, up, dz=1), step(over_chan, side_down, dz=-1)
        pieces = [mine, side, up, down, side_up, side_down, far, side_far]
        pieces = pieces + [step(over_chan, r, dc=1) for r in pieces]
        ch = lax.axis_index("chan")
        z, h, c = ch // 4, (ch // 2) % 2, ch % 2
        places = [((z + dz) % 4) * 4 + ((h + dh) % 2) * 2 + (c + dc) % 2 for dc in range(2) for dz, dh in ring_order]

        out = None
        for take in ((0, 8, 1, 9, 2, 10, 3, 11), (4, 12, 5, 13, 6, 14, 7, 15)):
            at = jnp.stack([places[n] for n in take]).astype(jnp.int32)
            out = pair_call(at, sources, [pieces[n] for n in take], high, low, 16, out)
        return out

    return jax.shard_map(
        stages,
        mesh=mesh,
        in_specs=(P("win", "chan", None), P("win", "chan")),
        out_specs=P("chan", None, "win", None, None),
        check_vma=False,
    )
```

profile of v0, /device:TPU:0, one launch (start us, length us, event | category | flops | bytes accessed | tf_op | source)
XLA Modules:
  0.0 117.8 jit_solution(3369422516104312167)
XLA Ops:
  0.0 5.7 %spectra.1 = (bf16[129,16,128]{2,1,0:T(8,128)(2,1)}, bf16[8,17,16,128]{3,2,1,0:T(8,128)(2,1)}) custom-call(bf16[1500,8,128]{2,1,0:T(8,128)(2,1)} %bitcast.25, s32[8,128]{1,0:T(8,128)} %v_ref.1, bf16[256,1536]{1,0:T(8,128)(2,1)} %constant.232.clone.t_ref), custom_call_target="tpu_custom_call" | custom-call | tf_op jit(solution)/shard_map/spectra/pallas_call | solution.py:99
  5.7 3.1 %collective-permute-start.2 = (bf16[129,16,128]{2,1,0:T(8,128)(2,1)}, bf16[129,16,128]{2,1,0:T(8,128)(2,1)S(1)}, u32[]{:S(2)}, u32[]{:S(2)}) collective-permute-start(bf16[129,16,128]{2,1,0:T(8,128)(2,1)} %get-tuple-element.7.refs_0_), channel_id=1, source_target_pairs={{0,6},{1,7},{2,0},{3,1},{4,2},{5,3},{6,4},{7,5},{8,14},{9,15},{10,... | collective-permute-start | bytes 1585160 | tf_op jit(solution)/shard_map/ppermute | solution.py:290
  8.9 0.0 collective-permute-start.1
  8.9 5.4 %all-to-all-start = ((bf16[8,17,16,128]{3,2,1,0:T(8,128)(2,1)}), bf16[8,17,16,128]{3,2,1,0:T(8,128)(2,1)S(1)}, u32[]{:S(2)}, u32[]{:S(2)}) async-start(bf16[8,17,16,128]{3,2,1,0:T(8,128)(2,1)} %get-tuple-element.8), calls=%async_computation | async-start | bytes 1114112 | tf_op jit(solution)/shard_map/all_to_all | solution.py:300
  14.3 2.0 %collective-permute-start = (bf16[129,16,128]{2,1,0:T(8,128)(2,1)}, bf16[129,16,128]{2,1,0:T(8,128)(2,1)S(1)}, u32[]{:S(2)}, u32[]{:S(2)}) collective-permute-start(bf16[129,16,128]{2,1,0:T(8,128)(2,1)} %get-tuple-element.7.refs_0_), channel_id=1, source_target_pairs={{0,1},{1,0},{2,3},{3,2},{4,5},{5,4},{6,7},{7,6},{8,9},{9,8},{10,11... | collective-permute-start | bytes 1585160 | tf_op jit(solution)/shard_map/ppermute | solution.py:290
  16.3 0.6 stack.98.order_ref
  17.0 12.8 %all-to-all-done.p_ref = bf16[8,17,16,128]{3,2,1,0:T(8,128)(2,1)S(1)} async-done(((bf16[8,17,16,128]{3,2,1,0:T(8,128)(2,1)}), bf16[8,17,16,128]{3,2,1,0:T(8,128)(2,1)S(1)}, u32[]{:S(2)}, u32[]{:S(2)}) %all-to-all-start) | async-done | bytes 557088 | tf_op jit(solution)/shard_map/all_to_all | solution.py:300
  29.7 0.8 copy-done
  30.5 4.0 %slot.1.refs_8_ = bf16[129,16,128]{2,1,0:T(8,128)(2,1)} custom-call(s32[8]{0:T(128)} %stack.98.order_ref, bf16[8,17,16,128]{3,2,1,0:T(8,128)(2,1)} %copy-done), custom_call_target="tpu_custom_call" | custom-call | tf_op jit(solution)/shard_map/slot/pallas_call | solution.py:150
  34.5 4.0 %collective-permute-start.20 = (bf16[129,16,128]{2,1,0:T(8,128)(2,1)}, bf16[129,16,128]{2,1,0:T(8,128)(2,1)S(1)}, u32[]{:S(2)}, u32[]{:S(2)}) collective-permute-start(bf16[129,16,128]{2,1,0:T(8,128)(2,1)} %slot.1.refs_8_), channel_id=1, source_target_pairs={{0,96},{8,104},{16,112},{24,120},{32,0},{40,8},{48,16},{56,24},{64... | collective-permute-start | bytes 1585160 | tf_op jit(solution)/shard_map/ppermute | solution.py:286
  38.6 0.0 collective-permute-start.17
  38.6 0.0 collective-permute-done.2.refs_3_
  38.6 0.1 collective-permute-start.12
  38.7 0.0 collective-permute-done.1.refs_2_
  38.7 0.0 copy-start.2
  38.7 3.1 %collective-permute-start.7 = (bf16[129,16,128]{2,1,0:T(8,128)(2,1)}, bf16[129,16,128]{2,1,0:T(8,128)(2,1)S(1)}, u32[]{:S(2)}, u32[]{:S(2)}) collective-permute-start(bf16[129,16,128]{2,1,0:T(8,128)(2,1)} %slot.1.refs_8_), channel_id=1, source_target_pairs={{0,16},{8,24},{16,0},{24,8},{32,48},{40,56},{48,32},{56,40},{64,80... | collective-permute-start | bytes 1585160 | tf_op jit(solution)/shard_map/ppermute | solution.py:286
  41.8 0.0 collective-permute-done.refs_1_
  41.8 0.0 collective-permute-start.5
  41.8 6.5 %collective-permute-done.20.refs_14_ = bf16[129,16,128]{2,1,0:T(8,128)(2,1)S(1)} collective-permute-done((bf16[129,16,128]{2,1,0:T(8,128)(2,1)}, bf16[129,16,128]{2,1,0:T(8,128)(2,1)S(1)}, u32[]{:S(2)}, u32[]{:S(2)}) %collective-permute-start.20) | collective-permute-done | bytes 528416 | tf_op jit(solution)/shard_map/ppermute | solution.py:286
  48.3 1.3 %collective-permute-start.4 = (bf16[129,16,128]{2,1,0:T(8,128)(2,1)S(1)}, bf16[129,16,128]{2,1,0:T(8,128)(2,1)S(1)}, u32[]{:S(2)}, u32[]{:S(2)}) collective-permute-start(bf16[129,16,128]{2,1,0:T(8,128)(2,1)S(1)} %collective-permute-done.refs_1_), channel_id=1, source_target_pairs={{0,6},{1,7},{2,0},{3,1},{4,2},{5,3},{6,4},{7,5},{8,14},{9,15},{10,... | collective-permute-start | bytes 1585160 | tf_op jit(solution)/shard_map/ppermute | solution.py:290
  49.6 0.0 collective-permute-done.17.refs_9_
  49.6 0.7 collective-permute-start.3
  50.3 4.1 %collective-permute-done.12.refs_12_ = bf16[129,16,128]{2,1,0:T(8,128)(2,1)S(1)} collective-permute-done((bf16[129,16,128]{2,1,0:T(8,128)(2,1)}, bf16[129,16,128]{2,1,0:T(8,128)(2,1)S(1)}, u32[]{:S(2)}, u32[]{:S(2)}) %collective-permute-start.12) | collective-permute-done | bytes 528416 | tf_op jit(solution)/shard_map/ppermute | solution.py:286
  54.4 0.0 collective-permute-start.21
  54.4 0.4 collective-permute-done.7.refs_10_
  54.8 2.9 %collective-permute-start.10 = (bf16[129,16,128]{2,1,0:T(8,128)(2,1)S(1)}, bf16[129,16,128]{2,1,0:T(8,128)(2,1)}, u32[]{:S(2)}, u32[]{:S(2)}) collective-permute-start(bf16[129,16,128]{2,1,0:T(8,128)(2,1)S(1)} %collective-permute-done.7.refs_10_), channel_id=1, source_target_pairs={{0,96},{8,104},{16,112},{24,120},{32,0},{40,8},{48,16},{56,24},{64... | collective-permute-start | bytes 1585160 | tf_op jit(solution)/shard_map/ppermute | solution.py:286
  57.7 0.2 collective-permute-done.5.refs_6_
  57.9 0.0 collective-permute-start.19
  57.9 1.4 %collective-permute-done.4.refs_5_ = bf16[129,16,128]{2,1,0:T(8,128)(2,1)S(1)} collective-permute-done((bf16[129,16,128]{2,1,0:T(8,128)(2,1)S(1)}, bf16[129,16,128]{2,1,0:T(8,128)(2,1)S(1)}, u32[]{:S(2)}, u32[]{:S(2)}) %collective-permute-start.4) | collective-permute-done | bytes 528416 | tf_op jit(solution)/shard_map/ppermute | solution.py:290
  59.3 0.6 collective-permute-start.13
  59.9 8.5 %collective-permute-done.3.refs_4_ = bf16[129,16,128]{2,1,0:T(8,128)(2,1)S(1)} collective-permute-done((bf16[129,16,128]{2,1,0:T(8,128)(2,1)S(1)}, bf16[129,16,128]{2,1,0:T(8,128)(2,1)S(1)}, u32[]{:S(2)}, u32[]{:S(2)}) %collective-permute-start.3) | collective-permute-done | bytes 528416 | tf_op jit(solution)/shard_map/ppermute | solution.py:290
  68.4 0.0 collective-permute-start.18
  68.4 0.0 collective-permute-done.21.refs_15_
  68.4 0.0 copy-start.10
  68.4 0.1 collective-permute-start.8
  68.5 0.5 collective-permute-done.10.refs_10_
  69.0 3.2 %collective-permute-start.15 = (bf16[129,16,128]{2,1,0:T(8,128)(2,1)}, bf16[129,16,128]{2,1,0:T(8,128)(2,1)}, u32[]{:S(2)}, u32[]{:S(2)}) collective-permute-start(bf16[129,16,128]{2,1,0:T(8,128)(2,1)} %collective-permute-done.10.refs_10_), channel_id=1, source_target_pairs={{0,96},{8,104},{16,112},{24,120},{32,0},{40,8},{48,16},{56,24},{64... | collective-permute-start | bytes 1585160 | tf_op jit(solution)/shard_map/ppermute | solution.py:286
  72.2 0.0 copy-done.7
  72.2 0.0 collective-permute-done.19.refs_13_
  72.2 0.0 copy-done.8
  72.2 0.0 copy-start.11
  72.2 0.3 collective-permute-start.6
  72.6 2.2 %collective-permute-done.13.refs_12_ = bf16[129,16,128]{2,1,0:T(8,128)(2,1)} collective-permute-done((bf16[129,16,128]{2,1,0:T(8,128)(2,1)S(1)}, bf16[129,16,128]{2,1,0:T(8,128)(2,1)}, u32[]{:S(2)}, u32[]{:S(2)}) %collective-permute-start.13) | collective-permute-done | bytes 528416 | tf_op jit(solution)/shard_map/ppermute | solution.py:286
  74.8 0.0 copy-done.9
  74.8 0.0 collective-permute-start.11
  74.8 0.0 collective-permute-done.18.refs_11_
  74.8 0.0 copy-start.12
  74.8 0.5 collective-permute-start.14
  75.3 9.8 %collective-permute-done.8.refs_8_ = bf16[129,16,128]{2,1,0:T(8,128)(2,1)} collective-permute-done((bf16[129,16,128]{2,1,0:T(8,128)(2,1)S(1)}, bf16[129,16,128]{2,1,0:T(8,128)(2,1)}, u32[]{:S(2)}, u32[]{:S(2)}) %collective-permute-start.8) | collective-permute-done | bytes 528416 | tf_op jit(solution)/shard_map/ppermute | solution.py:286
  85.2 0.0 copy-done.10
  85.2 0.0 collective-permute-start.9
  85.2 0.0 copy-done.11
  85.2 0.0 collective-permute-done.15.refs_14_
  85.2 0.8 collective-permute-start.16
  85.9 0.6 stack.89.place_ref
  86.6 0.6 stack.107.place_ref
  87.1 0.0 collective-permute-done.6.refs_7_
  87.1 0.0 copy-done.2
  87.2 15.2 %shard_map.55.refs_18_ = f32[128,16,1,16,128]{4,3,2,1,0:T(8,128)} custom-call(s32[8]{0:T(128)} %stack.107.place_ref, bf16[129,16,128]{2,1,0:T(8,128)(2,1)} %get-tuple-element.7.refs_0_, bf16[129,16,128]{2,1,0:T(8,128)(2,1)} %copy-done.3, bf16[129,16,128]{2,1,0:T(8,128)(2,1)} %copy-done.2, bf16[129,16,128]{2,1,0:T(8,128)(2,1)} %copy-done.1, ...), custom_call_target="tpu_custom_call" | custom-call | flops 4303355904 | bytes 8454144 | tf_op jit(solution)/shard_map/pallas_call | solution.py:254
  102.4 0.0 collective-permute-done.14.refs_13_
  102.4 0.0 collective-permute-done.11.refs_11_
  102.4 0.0 collective-permute-done.9.refs_9_
  102.4 0.0 collective-permute-done.16.refs_15_
  102.4 15.2 %shard_map.56 = f32[128,16,1,16,128]{4,3,2,1,0:T(8,128)} custom-call(s32[8]{0:T(128)} %stack.89.place_ref, bf16[129,16,128]{2,1,0:T(8,128)(2,1)} %get-tuple-element.7.refs_0_, bf16[129,16,128]{2,1,0:T(8,128)(2,1)} %copy-done.3, bf16[129,16,128]{2,1,0:T(8,128)(2,1)} %copy-done.2, bf16[129,16,128]{2,1,0:T(8,128)(2,1)} %copy-done.1, ...), custom_call_target="tpu_custom_call", output_to_operand_aliasing={{}: (19, {})} | custom-call | flops 4303355904 | bytes 8454144 | tf_op jit(solution)/shard_map/pallas_call | solution.py:254
  (15 shorter events, 0.0 us)
Async XLA Ops:
  5.7 32.9 %collective-permute-start.2 = (bf16[129,16,128]{2,1,0:T(8,128)(2,1)}, bf16[129,16,128]{2,1,0:T(8,128)(2,1)S(1)}, u32[]{:S(2)}, u32[]{:S(2)}) collective-permute-start(bf16[129,16,128]{2,1,0:T(8,128)(2,1)} %get-tuple-element.7.refs_0_), channel_id=1, source_target_pairs={{0,6},{1,7},{2,0},{3,1},{4,2},{5,3},{6,4},{7,5},{8,14},{9,15},{10,... | collective-permute-start | bytes 1585160 | tf_op jit(solution)/shard_map/ppermute | solution.py:290
  8.9 29.8 %collective-permute-start.1 = (bf16[129,16,128]{2,1,0:T(8,128)(2,1)}, bf16[129,16,128]{2,1,0:T(8,128)(2,1)S(1)}, u32[]{:S(2)}, u32[]{:S(2)}) collective-permute-start(bf16[129,16,128]{2,1,0:T(8,128)(2,1)} %get-tuple-element.7.refs_0_), channel_id=1, source_target_pairs={{0,2},{1,3},{2,4},{3,5},{4,6},{5,7},{6,0},{7,1},{8,10},{9,11},{10,... | collective-permute-start | bytes 1585160 | tf_op jit(solution)/shard_map/ppermute | solution.py:290
  8.9 20.9 %all-to-all-start = ((bf16[8,17,16,128]{3,2,1,0:T(8,128)(2,1)}), bf16[8,17,16,128]{3,2,1,0:T(8,128)(2,1)S(1)}, u32[]{:S(2)}, u32[]{:S(2)}) async-start(bf16[8,17,16,128]{3,2,1,0:T(8,128)(2,1)} %get-tuple-element.8), calls=%async_computation | async-start | bytes 1114112 | tf_op jit(solution)/shard_map/all_to_all | solution.py:300
  14.3 27.5 %collective-permute-start = (bf16[129,16,128]{2,1,0:T(8,128)(2,1)}, bf16[129,16,128]{2,1,0:T(8,128)(2,1)S(1)}, u32[]{:S(2)}, u32[]{:S(2)}) collective-permute-start(bf16[129,16,128]{2,1,0:T(8,128)(2,1)} %get-tuple-element.7.refs_0_), channel_id=1, source_target_pairs={{0,1},{1,0},{2,3},{3,2},{4,5},{5,4},{6,7},{7,6},{8,9},{9,8},{10,11... | collective-permute-start | bytes 1585160 | tf_op jit(solution)/shard_map/ppermute | solution.py:290
  29.7 0.8 copy-start
  34.5 13.7 %collective-permute-start.20 = (bf16[129,16,128]{2,1,0:T(8,128)(2,1)}, bf16[129,16,128]{2,1,0:T(8,128)(2,1)S(1)}, u32[]{:S(2)}, u32[]{:S(2)}) collective-permute-start(bf16[129,16,128]{2,1,0:T(8,128)(2,1)} %slot.1.refs_8_), channel_id=1, source_target_pairs={{0,96},{8,104},{16,112},{24,120},{32,0},{40,8},{48,16},{56,24},{64... | collective-permute-start | bytes 1585160 | tf_op jit(solution)/shard_map/ppermute | solution.py:286
  38.6 11.0 %collective-permute-start.17 = (bf16[129,16,128]{2,1,0:T(8,128)(2,1)}, bf16[129,16,128]{2,1,0:T(8,128)(2,1)}, u32[]{:S(2)}, u32[]{:S(2)}) collective-permute-start(bf16[129,16,128]{2,1,0:T(8,128)(2,1)} %slot.1.refs_8_), channel_id=1, source_target_pairs={{0,8},{8,0},{16,24},{24,16},{32,40},{40,32},{48,56},{56,48},{64,72... | collective-permute-start | bytes 1585160 | tf_op jit(solution)/shard_map/ppermute | solution.py:286
  38.6 48.5 %copy-start.1 = (bf16[129,16,128]{2,1,0:T(8,128)(2,1)}, bf16[129,16,128]{2,1,0:T(8,128)(2,1)S(1)}, u32[]{:S(2)}) copy-start(bf16[129,16,128]{2,1,0:T(8,128)(2,1)S(1)} %collective-permute-done.2.refs_3_) | copy-start | bytes 1585156
  38.6 15.8 %collective-permute-start.12 = (bf16[129,16,128]{2,1,0:T(8,128)(2,1)}, bf16[129,16,128]{2,1,0:T(8,128)(2,1)S(1)}, u32[]{:S(2)}, u32[]{:S(2)}) collective-permute-start(bf16[129,16,128]{2,1,0:T(8,128)(2,1)} %slot.1.refs_8_), channel_id=1, source_target_pairs={{0,32},{8,40},{16,48},{24,56},{32,64},{40,72},{48,80},{56,88},{64,... | collective-permute-start | bytes 1585160 | tf_op jit(solution)/shard_map/ppermute | solution.py:286
  38.7 48.4 %copy-start.2 = (bf16[129,16,128]{2,1,0:T(8,128)(2,1)}, bf16[129,16,128]{2,1,0:T(8,128)(2,1)S(1)}, u32[]{:S(2)}) copy-start(bf16[129,16,128]{2,1,0:T(8,128)(2,1)S(1)} %collective-permute-done.1.refs_2_) | copy-start | bytes 1585156
  38.7 16.1 %collective-permute-start.7 = (bf16[129,16,128]{2,1,0:T(8,128)(2,1)}, bf16[129,16,128]{2,1,0:T(8,128)(2,1)S(1)}, u32[]{:S(2)}, u32[]{:S(2)}) collective-permute-start(bf16[129,16,128]{2,1,0:T(8,128)(2,1)} %slot.1.refs_8_), channel_id=1, source_target_pairs={{0,16},{8,24},{16,0},{24,8},{32,48},{40,56},{48,32},{56,40},{64,80... | collective-permute-start | bytes 1585160 | tf_op jit(solution)/shard_map/ppermute | solution.py:286
  41.8 45.3 %copy-start.3 = (bf16[129,16,128]{2,1,0:T(8,128)(2,1)}, bf16[129,16,128]{2,1,0:T(8,128)(2,1)S(1)}, u32[]{:S(2)}) copy-start(bf16[129,16,128]{2,1,0:T(8,128)(2,1)S(1)} %collective-permute-done.refs_1_) | copy-start | bytes 1585156
  41.8 16.1 %collective-permute-start.5 = (bf16[129,16,128]{2,1,0:T(8,128)(2,1)S(1)}, bf16[129,16,128]{2,1,0:T(8,128)(2,1)S(1)}, u32[]{:S(2)}, u32[]{:S(2)}) collective-permute-start(bf16[129,16,128]{2,1,0:T(8,128)(2,1)S(1)} %collective-permute-done.1.refs_2_), channel_id=1, source_target_pairs={{0,2},{1,3},{2,4},{3,5},{4,6},{5,7},{6,0},{7,1},{8,10},{9,11},{10,... | collective-permute-start | bytes 1585160 | tf_op jit(solution)/shard_map/ppermute | solution.py:290
  48.3 23.9 %copy-start.7 = (bf16[129,16,128]{2,1,0:T(8,128)(2,1)}, bf16[129,16,128]{2,1,0:T(8,128)(2,1)S(1)}, u32[]{:S(2)}) copy-start(bf16[129,16,128]{2,1,0:T(8,128)(2,1)S(1)} %collective-permute-done.20.refs_14_) | copy-start | bytes 1585156
  48.3 11.0 %collective-permute-start.4 = (bf16[129,16,128]{2,1,0:T(8,128)(2,1)S(1)}, bf16[129,16,128]{2,1,0:T(8,128)(2,1)S(1)}, u32[]{:S(2)}, u32[]{:S(2)}) collective-permute-start(bf16[129,16,128]{2,1,0:T(8,128)(2,1)S(1)} %collective-permute-done.refs_1_), channel_id=1, source_target_pairs={{0,6},{1,7},{2,0},{3,1},{4,2},{5,3},{6,4},{7,5},{8,14},{9,15},{10,... | collective-permute-start | bytes 1585160 | tf_op jit(solution)/shard_map/ppermute | solution.py:290
  49.6 18.8 %collective-permute-start.3 = (bf16[129,16,128]{2,1,0:T(8,128)(2,1)S(1)}, bf16[129,16,128]{2,1,0:T(8,128)(2,1)S(1)}, u32[]{:S(2)}, u32[]{:S(2)}) collective-permute-start(bf16[129,16,128]{2,1,0:T(8,128)(2,1)S(1)} %collective-permute-done.refs_1_), channel_id=1, source_target_pairs={{0,2},{1,3},{2,4},{3,5},{4,6},{5,7},{6,0},{7,1},{8,10},{9,11},{10,... | collective-permute-start | bytes 1585160 | tf_op jit(solution)/shard_map/ppermute | solution.py:290
  54.4 17.8 %copy-start.8 = (bf16[129,16,128]{2,1,0:T(8,128)(2,1)}, bf16[129,16,128]{2,1,0:T(8,128)(2,1)S(1)}, u32[]{:S(2)}) copy-start(bf16[129,16,128]{2,1,0:T(8,128)(2,1)S(1)} %collective-permute-done.12.refs_12_) | copy-start | bytes 1585156
  54.4 14.0 %collective-permute-start.21 = (bf16[129,16,128]{2,1,0:T(8,128)(2,1)S(1)}, bf16[129,16,128]{2,1,0:T(8,128)(2,1)S(1)}, u32[]{:S(2)}, u32[]{:S(2)}) collective-permute-start(bf16[129,16,128]{2,1,0:T(8,128)(2,1)S(1)} %collective-permute-done.20.refs_14_), channel_id=1, source_target_pairs={{0,8},{8,0},{16,24},{24,16},{32,40},{40,32},{48,56},{56,48},{64,72... | collective-permute-start | bytes 1585160 | tf_op jit(solution)/shard_map/ppermute | solution.py:286
  54.8 20.0 %copy-start.9 = (bf16[129,16,128]{2,1,0:T(8,128)(2,1)}, bf16[129,16,128]{2,1,0:T(8,128)(2,1)S(1)}, u32[]{:S(2)}) copy-start(bf16[129,16,128]{2,1,0:T(8,128)(2,1)S(1)} %collective-permute-done.7.refs_10_) | copy-start | bytes 1585156
  54.8 14.1 %collective-permute-start.10 = (bf16[129,16,128]{2,1,0:T(8,128)(2,1)S(1)}, bf16[129,16,128]{2,1,0:T(8,128)(2,1)}, u32[]{:S(2)}, u32[]{:S(2)}) collective-permute-start(bf16[129,16,128]{2,1,0:T(8,128)(2,1)S(1)} %collective-permute-done.7.refs_10_), channel_id=1, source_target_pairs={{0,96},{8,104},{16,112},{24,120},{32,0},{40,8},{48,16},{56,24},{64... | collective-permute-start | bytes 1585160 | tf_op jit(solution)/shard_map/ppermute | solution.py:286
  57.9 29.2 %copy-start.4 = (bf16[129,16,128]{2,1,0:T(8,128)(2,1)}, bf16[129,16,128]{2,1,0:T(8,128)(2,1)S(1)}, u32[]{:S(2)}) copy-start(bf16[129,16,128]{2,1,0:T(8,128)(2,1)S(1)} %collective-permute-done.5.refs_6_) | copy-start | bytes 1585156
  57.9 14.3 %collective-permute-start.19 = (bf16[129,16,128]{2,1,0:T(8,128)(2,1)S(1)}, bf16[129,16,128]{2,1,0:T(8,128)(2,1)S(1)}, u32[]{:S(2)}, u32[]{:S(2)}) collective-permute-start(bf16[129,16,128]{2,1,0:T(8,128)(2,1)S(1)} %collective-permute-done.12.refs_12_), channel_id=1, source_target_pairs={{0,8},{8,0},{16,24},{24,16},{32,40},{40,32},{48,56},{56,48},{64,72... | collective-permute-start | bytes 1585160 | tf_op jit(solution)/shard_map/ppermute | solution.py:286
  59.3 27.9 %copy-start.5 = (bf16[129,16,128]{2,1,0:T(8,128)(2,1)}, bf16[129,16,128]{2,1,0:T(8,128)(2,1)S(1)}, u32[]{:S(2)}) copy-start(bf16[129,16,128]{2,1,0:T(8,128)(2,1)S(1)} %collective-permute-done.4.refs_5_) | copy-start | bytes 1585156
  59.3 15.5 %collective-permute-start.13 = (bf16[129,16,128]{2,1,0:T(8,128)(2,1)S(1)}, bf16[129,16,128]{2,1,0:T(8,128)(2,1)}, u32[]{:S(2)}, u32[]{:S(2)}) collective-permute-start(bf16[129,16,128]{2,1,0:T(8,128)(2,1)S(1)} %collective-permute-done.12.refs_12_), channel_id=1, source_target_pairs={{0,32},{8,40},{16,48},{24,56},{32,64},{40,72},{48,80},{56,88},{64,... | collective-permute-start | bytes 1585160 | tf_op jit(solution)/shard_map/ppermute | solution.py:286
  68.4 18.8 %copy-start.6 = (bf16[129,16,128]{2,1,0:T(8,128)(2,1)}, bf16[129,16,128]{2,1,0:T(8,128)(2,1)S(1)}, u32[]{:S(2)}) copy-start(bf16[129,16,128]{2,1,0:T(8,128)(2,1)S(1)} %collective-permute-done.3.refs_4_) | copy-start | bytes 1585156
  68.4 6.4 %collective-permute-start.18 = (bf16[129,16,128]{2,1,0:T(8,128)(2,1)S(1)}, bf16[129,16,128]{2,1,0:T(8,128)(2,1)S(1)}, u32[]{:S(2)}, u32[]{:S(2)}) collective-permute-start(bf16[129,16,128]{2,1,0:T(8,128)(2,1)S(1)} %collective-permute-done.7.refs_10_), channel_id=1, source_target_pairs={{0,8},{8,0},{16,24},{24,16},{32,40},{40,32},{48,56},{56,48},{64,72... | collective-permute-start | bytes 1585160 | tf_op jit(solution)/shard_map/ppermute | solution.py:286
  68.4 16.7 %copy-start.10 = (bf16[129,16,128]{2,1,0:T(8,128)(2,1)}, bf16[129,16,128]{2,1,0:T(8,128)(2,1)S(1)}, u32[]{:S(2)}) copy-start(bf16[129,16,128]{2,1,0:T(8,128)(2,1)S(1)} %collective-permute-done.21.refs_15_) | copy-start | bytes 1585156
  68.4 16.7 %collective-permute-start.8 = (bf16[129,16,128]{2,1,0:T(8,128)(2,1)S(1)}, bf16[129,16,128]{2,1,0:T(8,128)(2,1)}, u32[]{:S(2)}, u32[]{:S(2)}) collective-permute-start(bf16[129,16,128]{2,1,0:T(8,128)(2,1)S(1)} %collective-permute-done.7.refs_10_), channel_id=1, source_target_pairs={{0,32},{8,40},{16,48},{24,56},{32,64},{40,72},{48,80},{56,88},{64,... | collective-permute-start | bytes 1585160 | tf_op jit(solution)/shard_map/ppermute | solution.py:286
  69.0 16.2 %collective-permute-start.15 = (bf16[129,16,128]{2,1,0:T(8,128)(2,1)}, bf16[129,16,128]{2,1,0:T(8,128)(2,1)}, u32[]{:S(2)}, u32[]{:S(2)}) collective-permute-start(bf16[129,16,128]{2,1,0:T(8,128)(2,1)} %collective-permute-done.10.refs_10_), channel_id=1, source_target_pairs={{0,96},{8,104},{16,112},{24,120},{32,0},{40,8},{48,16},{56,24},{64... | collective-permute-start | bytes 1585160 | tf_op jit(solution)/shard_map/ppermute | solution.py:286
  72.2 12.9 %copy-start.11 = (bf16[129,16,128]{2,1,0:T(8,128)(2,1)}, bf16[129,16,128]{2,1,0:T(8,128)(2,1)S(1)}, u32[]{:S(2)}) copy-start(bf16[129,16,128]{2,1,0:T(8,128)(2,1)S(1)} %collective-permute-done.19.refs_13_) | copy-start | bytes 1585156
  72.2 14.9 %collective-permute-start.6 = (bf16[129,16,128]{2,1,0:T(8,128)(2,1)S(1)}, bf16[129,16,128]{2,1,0:T(8,128)(2,1)}, u32[]{:S(2)}, u32[]{:S(2)}) collective-permute-start(bf16[129,16,128]{2,1,0:T(8,128)(2,1)S(1)} %collective-permute-done.4.refs_5_), channel_id=1, source_target_pairs={{0,6},{1,7},{2,0},{3,1},{4,2},{5,3},{6,4},{7,5},{8,14},{9,15},{10,... | collective-permute-start | bytes 1585160 | tf_op jit(solution)/shard_map/ppermute | solution.py:290
  74.8 27.6 %collective-permute-start.11 = (bf16[129,16,128]{2,1,0:T(8,128)(2,1)}, bf16[129,16,128]{2,1,0:T(8,128)(2,1)}, u32[]{:S(2)}, u32[]{:S(2)}) collective-permute-start(bf16[129,16,128]{2,1,0:T(8,128)(2,1)} %collective-permute-done.10.refs_10_), channel_id=1, source_target_pairs={{0,8},{8,0},{16,24},{24,16},{32,40},{40,32},{48,56},{56,48},{64,72... | collective-permute-start | bytes 1585160 | tf_op jit(solution)/shard_map/ppermute | solution.py:286
  74.8 10.3 %copy-start.12 = (bf16[129,16,128]{2,1,0:T(8,128)(2,1)}, bf16[129,16,128]{2,1,0:T(8,128)(2,1)S(1)}, u32[]{:S(2)}) copy-start(bf16[129,16,128]{2,1,0:T(8,128)(2,1)S(1)} %collective-permute-done.18.refs_11_) | copy-start | bytes 1585156
  74.8 27.5 %collective-permute-start.14 = (bf16[129,16,128]{2,1,0:T(8,128)(2,1)}, bf16[129,16,128]{2,1,0:T(8,128)(2,1)}, u32[]{:S(2)}, u32[]{:S(2)}) collective-permute-start(bf16[129,16,128]{2,1,0:T(8,128)(2,1)} %collective-permute-done.13.refs_12_), channel_id=1, source_target_pairs={{0,8},{8,0},{16,24},{24,16},{32,40},{40,32},{48,56},{56,48},{64,72... | collective-permute-start | bytes 1585160 | tf_op jit(solution)/shard_map/ppermute | solution.py:286
  85.2 17.2 %collective-permute-start.9 = (bf16[129,16,128]{2,1,0:T(8,128)(2,1)}, bf16[129,16,128]{2,1,0:T(8,128)(2,1)}, u32[]{:S(2)}, u32[]{:S(2)}) collective-permute-start(bf16[129,16,128]{2,1,0:T(8,128)(2,1)} %collective-permute-done.8.refs_8_), channel_id=1, source_target_pairs={{0,8},{8,0},{16,24},{24,16},{32,40},{40,32},{48,56},{56,48},{64,72... | collective-permute-start | bytes 1585160 | tf_op jit(solution)/shard_map/ppermute | solution.py:286
  85.2 17.2 %collective-permute-start.16 = (bf16[129,16,128]{2,1,0:T(8,128)(2,1)}, bf16[129,16,128]{2,1,0:T(8,128)(2,1)}, u32[]{:S(2)}, u32[]{:S(2)}) collective-permute-start(bf16[129,16,128]{2,1,0:T(8,128)(2,1)} %collective-permute-done.15.refs_14_), channel_id=1, source_target_pairs={{0,8},{8,0},{16,24},{24,16},{32,40},{40,32},{48,56},{56,48},{64,72... | collective-permute-start | bytes 1585160 | tf_op jit(solution)/shard_map/ppermute | solution.py:286
where the time goes:
time: 119 us; the launch traced here: 118 us
  waiting for transfers between devices  46.4 us (39%)
  Pallas kernels  40.1 us (34%)
  starting transfers between devices  28.2 us (24%)
  local copies, waits for them, and re-layouts  2.66 us (2%)
    pallas_call x2, Pallas kernels, pair_call(): pl.pallas_call(kernel, grid_spec=pltpu.PrefetchScalarGridSpec(num_scalar_...  30.4 us
    ppermute x15, waiting for transfers between devices, over_chan(): return lax.ppermute(a, 'chan', perm)  23.5 us
    ppermute x15, starting transfers between devices, over_chan(): return lax.ppermute(a, 'chan', perm)  15.3 us
    all_to_all x1, waiting for transfers between devices, stages(): lax.all_to_all(slots, 'win', split_axis=0, concat_axis=0, tiled=True)  12.8 us
    ppermute x7, waiting for transfers between devices, over_win(): return lax.ppermute(a, 'win', perm)  10.1 us
    ppermute x7, starting transfers between devices, over_win(): return lax.ppermute(a, 'win', perm)  7.53 us
    pallas_call x1, Pallas kernels, spectra_call(): pl.pallas_call(kernel, grid=(steps,), in_specs=[pl.BlockSpec((SPAN, windo...  5.74 us
    all_to_all x1, starting transfers between devices, stages(): lax.all_to_all(slots, 'win', split_axis=0, concat_axis=0, tiled=True)  5.44 us
  transfers between devices with their start and end apart: 23, of which 10 were waited for; matrix products, arithmetic and copies ran while one was open for 2% of the time, Pallas kernels for 16%

commit v1 on v0

--- a/solution.py
+++ b/solution.py
@@ -18,7 +18,9 @@
 PITCH = 2 * BINS + 8
 ROW = 24
 SPAN = 512
-VMEM_LIMIT = 60 << 20
+PAIR_VMEM = 34 << 20
+SPECTRA_VMEM = 67043328
+SLOT_VMEM = 8 << 20
 
 
 def build_tables():
@@ -117,7 +119,7 @@
             pltpu.VMEM((windows // 2, 2 * BINS, 2 * channels), jnp.float32),
             pltpu.VMEM((BINS * 16, channels), jnp.float32),
         ],
-        compiler_params=pltpu.CompilerParams(dimension_semantics=("arbitrary",), vmem_limit_bytes=VMEM_LIMIT),
+        compiler_params=pltpu.CompilerParams(dimension_semantics=("arbitrary",), vmem_limit_bytes=SPECTRA_VMEM),
         name="spectra",
     )(by_time, validity, taper)
 
@@ -125,17 +127,26 @@
 def slot_call(order, parts):
     count, groups = parts.shape[:2]
 
-    span = 6
+    span = 9
     steps = pl.cdiv(groups, span)
     whole = groups - 1 - (steps - 1) * span
 
     def kernel(order_ref, p_ref, r_ref):
         g = pl.program_id(0)
 
+        lane = lax.broadcasted_iota(jnp.int32, (16, 128), 1)
+
         def body(b, _):
-            tiles = [p_ref[order_ref[q], b] for q in range(count)]
+            tiles = [p_ref[order_ref[q], b].astype(jnp.float32) for q in range(count)]
+            for d in (4, 2, 1):
+                low = (lane // (16 * d)) % 2 == 0
+                for q in range(8):
+                    if q & d == 0:
+                        one, two = tiles[q], tiles[q + d]
+                        tiles[q] = jnp.where(low, one, pltpu.roll(two, 16 * d, 1))
+                        tiles[q + d] = jnp.where(low, pltpu.roll(one, 128 - 16 * d, 1), two)
             for e in range(8):
-                r_ref[b * 8 + e] = jnp.concatenate([t[:, 16 * e : 16 * e + 16] for t in tiles], axis=1)
+                r_ref[b * 8 + e] = tiles[e].astype(jnp.bfloat16)
             return 0
 
         @pl.when(g < steps - 1)
@@ -156,12 +167,12 @@
             out_specs=pl.BlockSpec((span * 8, 16, 128), lambda g, o: (g, 0, 0)),
         ),
         out_shape=jax.ShapeDtypeStruct((ROWS, 16, 128), jnp.bfloat16),
-        compiler_params=pltpu.CompilerParams(dimension_semantics=("arbitrary",), vmem_limit_bytes=VMEM_LIMIT),
+        compiler_params=pltpu.CompilerParams(dimension_semantics=("arbitrary",), vmem_limit_bytes=SLOT_VMEM),
         name="slot",
     )(order, parts)
 
 
-def pair_call(places, sources, receivers, high, low, blocks, previous=None):
+def pair_call(places, base, sources, receivers, high, low, blocks, previous=None):
     count = len(receivers)
     rows = 16 * count
 
@@ -208,7 +219,7 @@
 
             def write(which, at):
                 return pltpu.make_async_copy(
-                    held.at[at, :, pl.ds(0, 16), :], out.at[:, place_ref[which], 0], sent.at[at]
+                    held.at[at, :, pl.ds(0, 16), :], out.at[:, place_ref[base + which], 0], sent.at[at]
                 )
 
             @pl.when(block >= 2)
@@ -267,7 +278,7 @@
         ),
         out_shape=jax.ShapeDtypeStruct((128, blocks, 1, 16, LAGS), jnp.float32),
         input_output_aliases=aliases,
-        compiler_params=pltpu.CompilerParams(dimension_semantics=("arbitrary",), vmem_limit_bytes=VMEM_LIMIT),
+        compiler_params=pltpu.CompilerParams(dimension_semantics=("arbitrary",), vmem_limit_bytes=PAIR_VMEM),
         cost_estimate=pl.CostEstimate(flops=2 * macs, bytes_accessed=(8 + count) * ROWS * 4096, transcendentals=0),
     )(places, *operands)
 
@@ -306,22 +317,22 @@
 
         w = lax.axis_index("win")
         y, x = w // 2, w % 2
-        order = jnp.stack([((y + dy) % 4) * 2 + (x + dx) % 2 for dy, dx in ring_order]).astype(jnp.int32)
-        mine = slot_call(order, parts)
+        ch = lax.axis_index("chan")
+        z, h, c = ch // 4, (ch // 2) % 2, ch % 2
+        order = [((y + dy) % 4) * 2 + (x + dx) % 2 for dy, dx in ring_order]
+        blocks = [((z + dz) % 4) * 4 + ((h + dh) % 2) * 2 + (c + dc) % 2 for dc in range(2) for dz, dh in ring_order]
+        first, second = (0, 8, 1, 9, 2, 10, 3, 11), (4, 12, 5, 13, 6, 14, 7, 15)
+        where = jnp.stack(order + [blocks[n] for n in first + second]).astype(jnp.int32)
+        mine = slot_call(where, parts)
         side = step(over_chan, mine, dh=1)
         up, down = step(over_chan, mine, dz=1), step(over_chan, mine, dz=-1)
         side_up, side_down = step(over_chan, side, dz=1), step(over_chan, side, dz=-1)
         far, side_far = step(over_chan, up, dz=1), step(over_chan, side_down, dz=-1)
         pieces = [mine, side, up, down, side_up, side_down, far, side_far]
         pieces = pieces + [step(over_chan, r, dc=1) for r in pieces]
-        ch = lax.axis_index("chan")
-        z, h, c = ch // 4, (ch // 2) % 2, ch % 2
-        places = [((z + dz) % 4) * 4 + ((h + dh) % 2) * 2 + (c + dc) % 2 for dc in range(2) for dz, dh in ring_order]
-
         out = None
-        for take in ((0, 8, 1, 9, 2, 10, 3, 11), (4, 12, 5, 13, 6, 14, 7, 15)):
-            at = jnp.stack([places[n] for n in take]).astype(jnp.int32)
-            out = pair_call(at, sources, [pieces[n] for n in take], high, low, 16, out)
+        for base, take in ((8, first), (16, second)):
+            out = pair_call(where, base, sources, [pieces[n] for n in take], high, low, 16, out)
         return out
 
     return jax.shard_map(

time: 119 us -> 113 us (0.950)
  Pallas kernels: 40.1 us -> 33.4 us
    pallas_call x2, Pallas kernels: 30.4 us -> 25.4 us  [pair_call(): pl.pallas_call(kernel, grid_spec=pltpu.PrefetchScalarGridSpec(num_scalar_...]
    unnamed x26 -> x6, local copies, waits for them, and re-layouts: 0.85 us -> 2.72 us
    pallas_call x1, Pallas kernels: 4.01 us -> 2.23 us  [slot_call(): pl.pallas_call(kernel, grid_spec=pltpu.PrefetchScalarGridSpec(num_scalar_...]
    another operation x3 -> x1, local copies, waits for them, and re-layouts: 1.81 us -> 0.1 us  [stages(): jnp.stack(order + [blocks[n] for n in first + second]).astype(jnp.int32)]
  transfers between devices with their start and end apart: 23 -> 23, of which waited for: 10 -> 10; matrix products, arithmetic and copies ran while one was open for 2% -> 0% of each run, Pallas kernels for 16% -> 13%
where the time goes in v1:
time: 113 us; the launch traced here: 111 us
  waiting for transfers between devices  46.8 us (41%)
  Pallas kernels  33.4 us (30%)
  starting transfers between devices  28 us (25%)
  local copies, waits for them, and re-layouts  2.82 us (2%)
    pallas_call x2, Pallas kernels, pair_call(): pl.pallas_call(kernel, grid_spec=pltpu.PrefetchScalarGridSpec(num_scalar_...  25.4 us
    ppermute x15, waiting for transfers between devices, over_chan(): return lax.ppermute(a, 'chan', perm)  23.3 us
    ppermute x15, starting transfers between devices, over_chan(): return lax.ppermute(a, 'chan', perm)  15.2 us
    all_to_all x1, waiting for transfers between devices, stages(): lax.all_to_all(slots, 'win', split_axis=0, concat_axis=0, tiled=True)  13.3 us
    ppermute x7, waiting for transfers between devices, over_win(): return lax.ppermute(a, 'win', perm)  10.2 us
    ppermute x7, starting transfers between devices, over_win(): return lax.ppermute(a, 'win', perm)  7.46 us
    pallas_call x1, Pallas kernels, spectra_call(): pl.pallas_call(kernel, grid=(steps,), in_specs=[pl.BlockSpec((SPAN, windo...  5.74 us
    all_to_all x1, starting transfers between devices, stages(): lax.all_to_all(slots, 'win', split_axis=0, concat_axis=0, tiled=True)  5.44 us
  transfers between devices with their start and end apart: 23, of which 10 were waited for; matrix products, arithmetic and copies ran while one was open for 0% of the time, Pallas kernels for 13%

profile of v1, /device:TPU:0, one launch (start us, length us, event | category | flops | bytes accessed | tf_op | source)
XLA Modules:
  0.0 111.4 jit_solution(2253043844084079816)
XLA Ops:
  0.0 5.7 %spectra.1 = (bf16[129,16,128]{2,1,0:T(8,128)(2,1)}, bf16[8,17,16,128]{3,2,1,0:T(8,128)(2,1)}) custom-call(bf16[1500,8,128]{2,1,0:T(8,128)(2,1)} %bitcast.25, s32[8,128]{1,0:T(8,128)} %v_ref.1, bf16[256,1536]{1,0:T(8,128)(2,1)} %constant.232.clone.t_ref), custom_call_target="tpu_custom_call" | custom-call | tf_op jit(solution)/shard_map/spectra/pallas_call | solution.py:101
  5.7 3.1 %collective-permute-start.2 = (bf16[129,16,128]{2,1,0:T(8,128)(2,1)}, bf16[129,16,128]{2,1,0:T(8,128)(2,1)S(1)}, u32[]{:S(2)}, u32[]{:S(2)}) collective-permute-start(bf16[129,16,128]{2,1,0:T(8,128)(2,1)} %get-tuple-element.7.refs_0_), channel_id=1, source_target_pairs={{0,6},{1,7},{2,0},{3,1},{4,2},{5,3},{6,4},{7,5},{8,14},{9,15},{10,... | collective-permute-start | bytes 1585160 | tf_op jit(solution)/shard_map/ppermute | solution.py:301
  8.9 0.0 collective-permute-start.1
  8.9 5.4 %all-to-all-start = ((bf16[8,17,16,128]{3,2,1,0:T(8,128)(2,1)}), bf16[8,17,16,128]{3,2,1,0:T(8,128)(2,1)S(1)}, u32[]{:S(2)}, u32[]{:S(2)}) async-start(bf16[8,17,16,128]{3,2,1,0:T(8,128)(2,1)} %get-tuple-element.8), calls=%async_computation | async-start | bytes 1114112 | tf_op jit(solution)/shard_map/all_to_all | solution.py:311
  14.3 2.0 %collective-permute-start = (bf16[129,16,128]{2,1,0:T(8,128)(2,1)}, bf16[129,16,128]{2,1,0:T(8,128)(2,1)S(1)}, u32[]{:S(2)}, u32[]{:S(2)}) collective-permute-start(bf16[129,16,128]{2,1,0:T(8,128)(2,1)} %get-tuple-element.7.refs_0_), channel_id=1, source_target_pairs={{0,1},{1,0},{2,3},{3,2},{4,5},{5,4},{6,7},{7,6},{8,9},{9,8},{10,11... | collective-permute-start | bytes 1585160 | tf_op jit(solution)/shard_map/ppermute | solution.py:301
  16.3 0.1 stack.99.order_ref.place_ref
  16.4 13.3 %all-to-all-done.p_ref = bf16[8,17,16,128]{3,2,1,0:T(8,128)(2,1)S(1)} async-done(((bf16[8,17,16,128]{3,2,1,0:T(8,128)(2,1)}), bf16[8,17,16,128]{3,2,1,0:T(8,128)(2,1)S(1)}, u32[]{:S(2)}, u32[]{:S(2)}) %all-to-all-start) | async-done | bytes 557088 | tf_op jit(solution)/shard_map/all_to_all | solution.py:311
  29.7 2.2 %slot.1.refs_8_ = bf16[129,16,128]{2,1,0:T(8,128)(2,1)S(1)} custom-call(s32[24]{0:T(128)S(1)} %stack.99.order_ref.place_ref, bf16[8,17,16,128]{3,2,1,0:T(8,128)(2,1)S(1)} %all-to-all-done.p_ref), custom_call_target="tpu_custom_call" | custom-call | tf_op jit(solution)/shard_map/slot/pallas_call | solution.py:161
  32.0 4.1 %collective-permute-start.20 = (bf16[129,16,128]{2,1,0:T(8,128)(2,1)S(1)}, bf16[129,16,128]{2,1,0:T(8,128)(2,1)S(1)}, u32[]{:S(2)}, u32[]{:S(2)}) collective-permute-start(bf16[129,16,128]{2,1,0:T(8,128)(2,1)S(1)} %slot.1.refs_8_), channel_id=1, source_target_pairs={{0,96},{8,104},{16,112},{24,120},{32,0},{40,8},{48,16},{56,24},{64... | collective-permute-start | bytes 1585160 | tf_op jit(solution)/shard_map/ppermute | solution.py:297
  36.1 0.0 collective-permute-start.17
  36.1 0.0 collective-permute-done.2.refs_3_
  36.1 0.0 collective-permute-start.12
  36.1 0.0 collective-permute-done.1.refs_2_
  36.1 3.1 %collective-permute-start.7 = (bf16[129,16,128]{2,1,0:T(8,128)(2,1)S(1)}, bf16[129,16,128]{2,1,0:T(8,128)(2,1)S(1)}, u32[]{:S(2)}, u32[]{:S(2)}) collective-permute-start(bf16[129,16,128]{2,1,0:T(8,128)(2,1)S(1)} %slot.1.refs_8_), channel_id=1, source_target_pairs={{0,16},{8,24},{16,0},{24,8},{32,48},{40,56},{48,32},{56,40},{64,80... | collective-permute-start | bytes 1585160 | tf_op jit(solution)/shard_map/ppermute | solution.py:297
  39.2 0.0 collective-permute-done.refs_1_
  39.2 0.0 collective-permute-start.5
  39.2 6.3 %collective-permute-done.20.refs_14_ = bf16[129,16,128]{2,1,0:T(8,128)(2,1)S(1)} collective-permute-done((bf16[129,16,128]{2,1,0:T(8,128)(2,1)S(1)}, bf16[129,16,128]{2,1,0:T(8,128)(2,1)S(1)}, u32[]{:S(2)}, u32[]{:S(2)}) %collective-permute-start.20) | collective-permute-done | bytes 528416 | tf_op jit(solution)/shard_map/ppermute | solution.py:297
  45.5 1.3 %collective-permute-start.4 = (bf16[129,16,128]{2,1,0:T(8,128)(2,1)S(1)}, bf16[129,16,128]{2,1,0:T(8,128)(2,1)S(1)}, u32[]{:S(2)}, u32[]{:S(2)}) collective-permute-start(bf16[129,16,128]{2,1,0:T(8,128)(2,1)S(1)} %collective-permute-done.refs_1_), channel_id=1, source_target_pairs={{0,6},{1,7},{2,0},{3,1},{4,2},{5,3},{6,4},{7,5},{8,14},{9,15},{10,... | collective-permute-start | bytes 1585160 | tf_op jit(solution)/shard_map/ppermute | solution.py:301
  46.8 0.0 collective-permute-done.17.refs_9_
  46.8 0.7 collective-permute-start.3
  47.5 4.2 %collective-permute-done.12.refs_12_ = bf16[129,16,128]{2,1,0:T(8,128)(2,1)S(1)} collective-permute-done((bf16[129,16,128]{2,1,0:T(8,128)(2,1)S(1)}, bf16[129,16,128]{2,1,0:T(8,128)(2,1)S(1)}, u32[]{:S(2)}, u32[]{:S(2)}) %collective-permute-start.12) | collective-permute-done | bytes 528416 | tf_op jit(solution)/shard_map/ppermute | solution.py:297
  51.7 0.0 collective-permute-start.21
  51.7 0.4 collective-permute-done.7.refs_10_
  52.1 2.9 %collective-permute-start.10 = (bf16[129,16,128]{2,1,0:T(8,128)(2,1)S(1)}, bf16[129,16,128]{2,1,0:T(8,128)(2,1)S(1)}, u32[]{:S(2)}, u32[]{:S(2)}) collective-permute-start(bf16[129,16,128]{2,1,0:T(8,128)(2,1)S(1)} %collective-permute-done.7.refs_10_), channel_id=1, source_target_pairs={{0,96},{8,104},{16,112},{24,120},{32,0},{40,8},{48,16},{56,24},{64... | collective-permute-start | bytes 1585160 | tf_op jit(solution)/shard_map/ppermute | solution.py:297
  55.0 0.3 collective-permute-done.5.refs_6_
  55.3 0.0 collective-permute-start.19
  55.3 1.2 %collective-permute-done.4.refs_5_ = bf16[129,16,128]{2,1,0:T(8,128)(2,1)S(1)} collective-permute-done((bf16[129,16,128]{2,1,0:T(8,128)(2,1)S(1)}, bf16[129,16,128]{2,1,0:T(8,128)(2,1)S(1)}, u32[]{:S(2)}, u32[]{:S(2)}) %collective-permute-start.4) | collective-permute-done | bytes 528416 | tf_op jit(solution)/shard_map/ppermute | solution.py:301
  56.5 0.7 collective-permute-start.13
  57.2 8.7 %collective-permute-done.3.refs_4_ = bf16[129,16,128]{2,1,0:T(8,128)(2,1)S(1)} collective-permute-done((bf16[129,16,128]{2,1,0:T(8,128)(2,1)S(1)}, bf16[129,16,128]{2,1,0:T(8,128)(2,1)S(1)}, u32[]{:S(2)}, u32[]{:S(2)}) %collective-permute-start.3) | collective-permute-done | bytes 528416 | tf_op jit(solution)/shard_map/ppermute | solution.py:301
  65.9 0.0 collective-permute-start.18
  65.9 0.0 collective-permute-done.21.refs_15_
  65.9 0.0 collective-permute-start.8
  65.9 0.3 collective-permute-done.10.refs_10_
  66.1 3.3 %collective-permute-start.15 = (bf16[129,16,128]{2,1,0:T(8,128)(2,1)S(1)}, bf16[129,16,128]{2,1,0:T(8,128)(2,1)S(1)}, u32[]{:S(2)}, u32[]{:S(2)}) collective-permute-start(bf16[129,16,128]{2,1,0:T(8,128)(2,1)S(1)} %collective-permute-done.10.refs_10_), channel_id=1, source_target_pairs={{0,96},{8,104},{16,112},{24,120},{32,0},{40,8},{48,16},{56,24},{64... | collective-permute-start | bytes 1585160 | tf_op jit(solution)/shard_map/ppermute | solution.py:297
  69.5 0.0 collective-permute-done.19.refs_13_
  69.5 0.3 collective-permute-start.6
  69.8 2.3 %collective-permute-done.13.refs_12_ = bf16[129,16,128]{2,1,0:T(8,128)(2,1)S(1)} collective-permute-done((bf16[129,16,128]{2,1,0:T(8,128)(2,1)S(1)}, bf16[129,16,128]{2,1,0:T(8,128)(2,1)S(1)}, u32[]{:S(2)}, u32[]{:S(2)}) %collective-permute-start.13) | collective-permute-done | bytes 528416 | tf_op jit(solution)/shard_map/ppermute | solution.py:297
  72.1 0.0 collective-permute-start.11
  72.1 0.0 collective-permute-done.18.refs_11_
  72.1 0.5 collective-permute-start.14
  72.6 9.9 %collective-permute-done.8.refs_8_ = bf16[129,16,128]{2,1,0:T(8,128)(2,1)S(1)} collective-permute-done((bf16[129,16,128]{2,1,0:T(8,128)(2,1)S(1)}, bf16[129,16,128]{2,1,0:T(8,128)(2,1)S(1)}, u32[]{:S(2)}, u32[]{:S(2)}) %collective-permute-start.8) | collective-permute-done | bytes 528416 | tf_op jit(solution)/shard_map/ppermute | solution.py:297
  82.5 0.0 collective-permute-start.9
  82.5 0.0 collective-permute-done.15.refs_14_
  82.5 0.5 collective-permute-start.16
  83.0 0.0 collective-permute-done.6.refs_7_
  83.0 0.0 copy-start
  83.0 1.0 copy-done
  84.0 0.0 copy-start.1
  84.0 0.8 copy-done.1
  84.9 0.0 copy-start.2
  84.9 0.8 copy-done.2
  85.7 12.7 %shard_map.55.refs_18_ = f32[128,16,1,16,128]{4,3,2,1,0:T(8,128)} custom-call(s32[24]{0:T(128)S(1)} %stack.99.order_ref.place_ref, bf16[129,16,128]{2,1,0:T(8,128)(2,1)S(1)} %copy-done, bf16[129,16,128]{2,1,0:T(8,128)(2,1)S(1)} %collective-permute-done.refs_1_, bf16[129,16,128]{2,1,0:T(8,128)(2,1)S(1)} %collective-permute-done.1.refs_2_, ...), custom_call_target="tpu_custom_call" | custom-call | flops 4303355904 | bytes 8454144 | tf_op jit(solution)/shard_map/pallas_call | solution.py:265
  98.4 0.0 collective-permute-done.14.refs_13_
  98.4 0.0 collective-permute-done.11.refs_11_
  98.4 0.0 collective-permute-done.9.refs_9_
  98.5 0.0 collective-permute-done.16.refs_15_
  98.5 12.7 %shard_map.56 = f32[128,16,1,16,128]{4,3,2,1,0:T(8,128)} custom-call(s32[24]{0:T(128)S(1)} %stack.99.order_ref.place_ref, bf16[129,16,128]{2,1,0:T(8,128)(2,1)S(1)} %copy-done, bf16[129,16,128]{2,1,0:T(8,128)(2,1)S(1)} %collective-permute-done.refs_1_, bf16[129,16,128]{2,1,0:T(8,128)(2,1)S(1)} %collective-permute-done.1.refs_2_, ...), custom_call_target="tpu_custom_call", output_to_operand_aliasing={{}: (19, {})} | custom-call | flops 4303355904 | bytes 8454144 | tf_op jit(solution)/shard_map/pallas_call | solution.py:265
Async XLA Ops:
  5.7 30.3 %collective-permute-start.2 = (bf16[129,16,128]{2,1,0:T(8,128)(2,1)}, bf16[129,16,128]{2,1,0:T(8,128)(2,1)S(1)}, u32[]{:S(2)}, u32[]{:S(2)}) collective-permute-start(bf16[129,16,128]{2,1,0:T(8,128)(2,1)} %get-tuple-element.7.refs_0_), channel_id=1, source_target_pairs={{0,6},{1,7},{2,0},{3,1},{4,2},{5,3},{6,4},{7,5},{8,14},{9,15},{10,... | collective-permute-start | bytes 1585160 | tf_op jit(solution)/shard_map/ppermute | solution.py:301
  8.9 27.2 %collective-permute-start.1 = (bf16[129,16,128]{2,1,0:T(8,128)(2,1)}, bf16[129,16,128]{2,1,0:T(8,128)(2,1)S(1)}, u32[]{:S(2)}, u32[]{:S(2)}) collective-permute-start(bf16[129,16,128]{2,1,0:T(8,128)(2,1)} %get-tuple-element.7.refs_0_), channel_id=1, source_target_pairs={{0,2},{1,3},{2,4},{3,5},{4,6},{5,7},{6,0},{7,1},{8,10},{9,11},{10,... | collective-permute-start | bytes 1585160 | tf_op jit(solution)/shard_map/ppermute | solution.py:301
  8.9 20.9 %all-to-all-start = ((bf16[8,17,16,128]{3,2,1,0:T(8,128)(2,1)}), bf16[8,17,16,128]{3,2,1,0:T(8,128)(2,1)S(1)}, u32[]{:S(2)}, u32[]{:S(2)}) async-start(bf16[8,17,16,128]{3,2,1,0:T(8,128)(2,1)} %get-tuple-element.8), calls=%async_computation | async-start | bytes 1114112 | tf_op jit(solution)/shard_map/all_to_all | solution.py:311
  14.3 24.9 %collective-permute-start = (bf16[129,16,128]{2,1,0:T(8,128)(2,1)}, bf16[129,16,128]{2,1,0:T(8,128)(2,1)S(1)}, u32[]{:S(2)}, u32[]{:S(2)}) collective-permute-start(bf16[129,16,128]{2,1,0:T(8,128)(2,1)} %get-tuple-element.7.refs_0_), channel_id=1, source_target_pairs={{0,1},{1,0},{2,3},{3,2},{4,5},{5,4},{6,7},{7,6},{8,9},{9,8},{10,11... | collective-permute-start | bytes 1585160 | tf_op jit(solution)/shard_map/ppermute | solution.py:301
  32.0 13.5 %collective-permute-start.20 = (bf16[129,16,128]{2,1,0:T(8,128)(2,1)S(1)}, bf16[129,16,128]{2,1,0:T(8,128)(2,1)S(1)}, u32[]{:S(2)}, u32[]{:S(2)}) collective-permute-start(bf16[129,16,128]{2,1,0:T(8,128)(2,1)S(1)} %slot.1.refs_8_), channel_id=1, source_target_pairs={{0,96},{8,104},{16,112},{24,120},{32,0},{40,8},{48,16},{56,24},{64... | collective-permute-start | bytes 1585160 | tf_op jit(solution)/shard_map/ppermute | solution.py:297
  36.1 10.7 %collective-permute-start.17 = (bf16[129,16,128]{2,1,0:T(8,128)(2,1)S(1)}, bf16[129,16,128]{2,1,0:T(8,128)(2,1)S(1)}, u32[]{:S(2)}, u32[]{:S(2)}) collective-permute-start(bf16[129,16,128]{2,1,0:T(8,128)(2,1)S(1)} %slot.1.refs_8_), channel_id=1, source_target_pairs={{0,8},{8,0},{16,24},{24,16},{32,40},{40,32},{48,56},{56,48},{64,72... | collective-permute-start | bytes 1585160 | tf_op jit(solution)/shard_map/ppermute | solution.py:297
  36.1 15.6 %collective-permute-start.12 = (bf16[129,16,128]{2,1,0:T(8,128)(2,1)S(1)}, bf16[129,16,128]{2,1,0:T(8,128)(2,1)S(1)}, u32[]{:S(2)}, u32[]{:S(2)}) collective-permute-start(bf16[129,16,128]{2,1,0:T(8,128)(2,1)S(1)} %slot.1.refs_8_), channel_id=1, source_target_pairs={{0,32},{8,40},{16,48},{24,56},{32,64},{40,72},{48,80},{56,88},{64,... | collective-permute-start | bytes 1585160 | tf_op jit(solution)/shard_map/ppermute | solution.py:297
  36.1 16.0 %collective-permute-start.7 = (bf16[129,16,128]{2,1,0:T(8,128)(2,1)S(1)}, bf16[129,16,128]{2,1,0:T(8,128)(2,1)S(1)}, u32[]{:S(2)}, u32[]{:S(2)}) collective-permute-start(bf16[129,16,128]{2,1,0:T(8,128)(2,1)S(1)} %slot.1.refs_8_), channel_id=1, source_target_pairs={{0,16},{8,24},{16,0},{24,8},{32,48},{40,56},{48,32},{56,40},{64,80... | collective-permute-start | bytes 1585160 | tf_op jit(solution)/shard_map/ppermute | solution.py:297
  39.2 16.1 %collective-permute-start.5 = (bf16[129,16,128]{2,1,0:T(8,128)(2,1)S(1)}, bf16[129,16,128]{2,1,0:T(8,128)(2,1)S(1)}, u32[]{:S(2)}, u32[]{:S(2)}) collective-permute-start(bf16[129,16,128]{2,1,0:T(8,128)(2,1)S(1)} %collective-permute-done.1.refs_2_), channel_id=1, source_target_pairs={{0,2},{1,3},{2,4},{3,5},{4,6},{5,7},{6,0},{7,1},{8,10},{9,11},{10,... | collective-permute-start | bytes 1585160 | tf_op jit(solution)/shard_map/ppermute | solution.py:301
  45.5 11.0 %collective-permute-start.4 = (bf16[129,16,128]{2,1,0:T(8,128)(2,1)S(1)}, bf16[129,16,128]{2,1,0:T(8,128)(2,1)S(1)}, u32[]{:S(2)}, u32[]{:S(2)}) collective-permute-start(bf16[129,16,128]{2,1,0:T(8,128)(2,1)S(1)} %collective-permute-done.refs_1_), channel_id=1, source_target_pairs={{0,6},{1,7},{2,0},{3,1},{4,2},{5,3},{6,4},{7,5},{8,14},{9,15},{10,... | collective-permute-start | bytes 1585160 | tf_op jit(solution)/shard_map/ppermute | solution.py:301
  46.8 19.1 %collective-permute-start.3 = (bf16[129,16,128]{2,1,0:T(8,128)(2,1)S(1)}, bf16[129,16,128]{2,1,0:T(8,128)(2,1)S(1)}, u32[]{:S(2)}, u32[]{:S(2)}) collective-permute-start(bf16[129,16,128]{2,1,0:T(8,128)(2,1)S(1)} %collective-permute-done.refs_1_), channel_id=1, source_target_pairs={{0,2},{1,3},{2,4},{3,5},{4,6},{5,7},{6,0},{7,1},{8,10},{9,11},{10,... | collective-permute-start | bytes 1585160 | tf_op jit(solution)/shard_map/ppermute | solution.py:301
  51.7 14.2 %collective-permute-start.21 = (bf16[129,16,128]{2,1,0:T(8,128)(2,1)S(1)}, bf16[129,16,128]{2,1,0:T(8,128)(2,1)S(1)}, u32[]{:S(2)}, u32[]{:S(2)}) collective-permute-start(bf16[129,16,128]{2,1,0:T(8,128)(2,1)S(1)} %collective-permute-done.20.refs_14_), channel_id=1, source_target_pairs={{0,8},{8,0},{16,24},{24,16},{32,40},{40,32},{48,56},{56,48},{64,72... | collective-permute-start | bytes 1585160 | tf_op jit(solution)/shard_map/ppermute | solution.py:297
  52.1 14.0 %collective-permute-start.10 = (bf16[129,16,128]{2,1,0:T(8,128)(2,1)S(1)}, bf16[129,16,128]{2,1,0:T(8,128)(2,1)S(1)}, u32[]{:S(2)}, u32[]{:S(2)}) collective-permute-start(bf16[129,16,128]{2,1,0:T(8,128)(2,1)S(1)} %collective-permute-done.7.refs_10_), channel_id=1, source_target_pairs={{0,96},{8,104},{16,112},{24,120},{32,0},{40,8},{48,16},{56,24},{64... | collective-permute-start | bytes 1585160 | tf_op jit(solution)/shard_map/ppermute | solution.py:297
  55.3 14.2 %collective-permute-start.19 = (bf16[129,16,128]{2,1,0:T(8,128)(2,1)S(1)}, bf16[129,16,128]{2,1,0:T(8,128)(2,1)S(1)}, u32[]{:S(2)}, u32[]{:S(2)}) collective-permute-start(bf16[129,16,128]{2,1,0:T(8,128)(2,1)S(1)} %collective-permute-done.12.refs_12_), channel_id=1, source_target_pairs={{0,8},{8,0},{16,24},{24,16},{32,40},{40,32},{48,56},{56,48},{64,72... | collective-permute-start | bytes 1585160 | tf_op jit(solution)/shard_map/ppermute | solution.py:297
  56.5 15.6 %collective-permute-start.13 = (bf16[129,16,128]{2,1,0:T(8,128)(2,1)S(1)}, bf16[129,16,128]{2,1,0:T(8,128)(2,1)S(1)}, u32[]{:S(2)}, u32[]{:S(2)}) collective-permute-start(bf16[129,16,128]{2,1,0:T(8,128)(2,1)S(1)} %collective-permute-done.12.refs_12_), channel_id=1, source_target_pairs={{0,32},{8,40},{16,48},{24,56},{32,64},{40,72},{48,80},{56,88},{64,... | collective-permute-start | bytes 1585160 | tf_op jit(solution)/shard_map/ppermute | solution.py:297
  65.9 6.2 %collective-permute-start.18 = (bf16[129,16,128]{2,1,0:T(8,128)(2,1)S(1)}, bf16[129,16,128]{2,1,0:T(8,128)(2,1)S(1)}, u32[]{:S(2)}, u32[]{:S(2)}) collective-permute-start(bf16[129,16,128]{2,1,0:T(8,128)(2,1)S(1)} %collective-permute-done.7.refs_10_), channel_id=1, source_target_pairs={{0,8},{8,0},{16,24},{24,16},{32,40},{40,32},{48,56},{56,48},{64,72... | collective-permute-start | bytes 1585160 | tf_op jit(solution)/shard_map/ppermute | solution.py:297
  65.9 16.6 %collective-permute-start.8 = (bf16[129,16,128]{2,1,0:T(8,128)(2,1)S(1)}, bf16[129,16,128]{2,1,0:T(8,128)(2,1)S(1)}, u32[]{:S(2)}, u32[]{:S(2)}) collective-permute-start(bf16[129,16,128]{2,1,0:T(8,128)(2,1)S(1)} %collective-permute-done.7.refs_10_), channel_id=1, source_target_pairs={{0,32},{8,40},{16,48},{24,56},{32,64},{40,72},{48,80},{56,88},{64,... | collective-permute-start | bytes 1585160 | tf_op jit(solution)/shard_map/ppermute | solution.py:297
  66.1 16.3 %collective-permute-start.15 = (bf16[129,16,128]{2,1,0:T(8,128)(2,1)S(1)}, bf16[129,16,128]{2,1,0:T(8,128)(2,1)S(1)}, u32[]{:S(2)}, u32[]{:S(2)}) collective-permute-start(bf16[129,16,128]{2,1,0:T(8,128)(2,1)S(1)} %collective-permute-done.10.refs_10_), channel_id=1, source_target_pairs={{0,96},{8,104},{16,112},{24,120},{32,0},{40,8},{48,16},{56,24},{64... | collective-permute-start | bytes 1585160 | tf_op jit(solution)/shard_map/ppermute | solution.py:297
  69.5 13.5 %collective-permute-start.6 = (bf16[129,16,128]{2,1,0:T(8,128)(2,1)S(1)}, bf16[129,16,128]{2,1,0:T(8,128)(2,1)S(1)}, u32[]{:S(2)}, u32[]{:S(2)}) collective-permute-start(bf16[129,16,128]{2,1,0:T(8,128)(2,1)S(1)} %collective-permute-done.4.refs_5_), channel_id=1, source_target_pairs={{0,6},{1,7},{2,0},{3,1},{4,2},{5,3},{6,4},{7,5},{8,14},{9,15},{10,... | collective-permute-start | bytes 1585160 | tf_op jit(solution)/shard_map/ppermute | solution.py:301
  72.1 26.4 %collective-permute-start.11 = (bf16[129,16,128]{2,1,0:T(8,128)(2,1)S(1)}, bf16[129,16,128]{2,1,0:T(8,128)(2,1)S(1)}, u32[]{:S(2)}, u32[]{:S(2)}) collective-permute-start(bf16[129,16,128]{2,1,0:T(8,128)(2,1)S(1)} %collective-permute-done.10.refs_10_), channel_id=1, source_target_pairs={{0,8},{8,0},{16,24},{24,16},{32,40},{40,32},{48,56},{56,48},{64,72... | collective-permute-start | bytes 1585160 | tf_op jit(solution)/shard_map/ppermute | solution.py:297
  72.1 26.4 %collective-permute-start.14 = (bf16[129,16,128]{2,1,0:T(8,128)(2,1)S(1)}, bf16[129,16,128]{2,1,0:T(8,128)(2,1)S(1)}, u32[]{:S(2)}, u32[]{:S(2)}) collective-permute-start(bf16[129,16,128]{2,1,0:T(8,128)(2,1)S(1)} %collective-permute-done.13.refs_12_), channel_id=1, source_target_pairs={{0,8},{8,0},{16,24},{24,16},{32,40},{40,32},{48,56},{56,48},{64,72... | collective-permute-start | bytes 1585160 | tf_op jit(solution)/shard_map/ppermute | solution.py:297
  82.5 16.0 %collective-permute-start.9 = (bf16[129,16,128]{2,1,0:T(8,128)(2,1)S(1)}, bf16[129,16,128]{2,1,0:T(8,128)(2,1)S(1)}, u32[]{:S(2)}, u32[]{:S(2)}) collective-permute-start(bf16[129,16,128]{2,1,0:T(8,128)(2,1)S(1)} %collective-permute-done.8.refs_8_), channel_id=1, source_target_pairs={{0,8},{8,0},{16,24},{24,16},{32,40},{40,32},{48,56},{56,48},{64,72... | collective-permute-start | bytes 1585160 | tf_op jit(solution)/shard_map/ppermute | solution.py:297
  82.5 16.0 %collective-permute-start.16 = (bf16[129,16,128]{2,1,0:T(8,128)(2,1)S(1)}, bf16[129,16,128]{2,1,0:T(8,128)(2,1)S(1)}, u32[]{:S(2)}, u32[]{:S(2)}) collective-permute-start(bf16[129,16,128]{2,1,0:T(8,128)(2,1)S(1)} %collective-permute-done.15.refs_14_), channel_id=1, source_target_pairs={{0,8},{8,0},{16,24},{24,16},{32,40},{40,32},{48,56},{56,48},{64,72... | collective-permute-start | bytes 1585160 | tf_op jit(solution)/shard_map/ppermute | solution.py:297
  83.0 1.0 copy-start
  84.0 0.8 copy-start.1
  84.9 0.8 copy-start.2

commit v2 on v1

--- a/solution.py
+++ b/solution.py
@@ -19,7 +19,7 @@
 ROW = 24
 SPAN = 512
 PAIR_VMEM = 34 << 20
-SPECTRA_VMEM = 67043328
+SPECTRA_VMEM = 67043328 - 1300000
 SLOT_VMEM = 8 << 20
 
 
@@ -36,7 +36,7 @@
     inverse = np.ascontiguousarray(inverse.T).astype(np.float32)
     high = inverse.astype(jnp.bfloat16)
     low = (inverse - high.astype(np.float32)).astype(jnp.bfloat16)
-    return taper, high, low
+    return taper, np.concatenate([high, low], axis=0)
 
 
 def spectra_call(series, validity, taper):
@@ -172,16 +172,26 @@
     )(order, parts)
 
 
-def pair_call(places, base, sources, receivers, high, low, blocks, previous=None):
+def pair_call(places, base, sources, receivers, lags, blocks, previous=None):
     count = len(receivers)
     rows = 16 * count
 
     def kernel(place_ref, *refs):
         src = refs[:8]
         rcv = refs[8 : 8 + count]
-        hi_ref, lo_ref = refs[8 + count : 10 + count]
-        out, joined, recip, held, sent = refs[-5:]
+        table_ref = refs[8 + count]
+        out, joined, recip, held, tables, sent, fetched = refs[-7:]
         g = pl.program_id(0)
+
+        fetch = pltpu.make_async_copy(table_ref, tables, fetched)
+
+        @pl.when(g == 0)
+        def _():
+            fetch.start()
+
+        @pl.when(g == STEPS)
+        def _():
+            fetch.wait()
 
         def one_bin(k):
             tiles = [s[k] for s in src]
@@ -235,9 +245,8 @@
                 pair = jnp.concatenate([joined[pl.ds(first, 256), :], joined[pl.ds(second, 256), :]], axis=1)
                 upper = pair.astype(jnp.bfloat16)
                 lower = (pair - upper.astype(jnp.float32)).astype(jnp.bfloat16)
-                tables = jnp.concatenate([hi_ref[...], lo_ref[...]], axis=0)
-                acc = jnp.dot(tables, upper, preferred_element_type=jnp.float32)
-                acc = acc[:LAGS] + acc[LAGS:] + jnp.dot(hi_ref[...], lower, preferred_element_type=jnp.float32)
+                acc = jnp.dot(tables[...], upper, preferred_element_type=jnp.float32)
+                acc = acc[:LAGS] + acc[LAGS:] + jnp.dot(tables[:LAGS], lower, preferred_element_type=jnp.float32)
                 scale = jnp.concatenate([recip[pl.ds(i, 1), :], recip[pl.ds(i + 1, 1), :]], axis=1)
                 acc = acc * scale
                 flat[pl.ds(2 * q, 128, stride=ROW), :] = acc[:, :128].T
@@ -253,9 +262,8 @@
                 write(block, slot).wait()
 
     piece = pl.BlockSpec((CHUNK, 16, 128), lambda g, at: (jnp.minimum(g, STEPS - 1), 0, 0))
-    table = pl.BlockSpec((LAGS, 2 * BINS), lambda g, at: (0, 0))
-    in_specs = [piece] * (8 + count) + [table] * 2
-    operands = [*sources, *receivers, high, low]
+    in_specs = [piece] * (8 + count) + [pl.BlockSpec(memory_space=pltpu.HBM)]
+    operands = [*sources, *receivers, lags]
     aliases = {}
     if previous is not None:
         in_specs.append(pl.BlockSpec(memory_space=pl.ANY))
@@ -273,7 +281,9 @@
                 pltpu.VMEM((rows * PITCH, 128), jnp.float32),
                 pltpu.VMEM((rows, 128), jnp.float32),
                 pltpu.VMEM((2, 128, ROW, LAGS), jnp.float32),
+                pltpu.VMEM((2 * LAGS, 2 * BINS), jnp.bfloat16),
                 pltpu.SemaphoreType.DMA((2,)),
+                pltpu.SemaphoreType.DMA,
             ],
         ),
         out_shape=jax.ShapeDtypeStruct((128, blocks, 1, 16, LAGS), jnp.float32),
@@ -284,7 +294,7 @@
 
 
 def solution(mesh):
-    taper, high, low = build_tables()
+    taper, lags = build_tables()
 
     def chan_of(z, h, c):
         return (z % 4) * 4 + (h % 2) * 2 + c % 2
@@ -332,7 +342,7 @@
         pieces = pieces + [step(over_chan, r, dc=1) for r in pieces]
         out = None
         for base, take in ((8, first), (16, second)):
-            out = pair_call(where, base, sources, [pieces[n] for n in take], high, low, 16, out)
+            out = pair_call(where, base, sources, [pieces[n] for n in take], lags, 16, out)
         return out
 
     return jax.shard_map(

time: 113 us -> 112 us (level)
    unnamed x6 -> x4, local copies, waits for them, and re-layouts: 2.72 us -> 1.95 us
  transfers between devices with their start and end apart: 23 -> 23, of which waited for: 10 -> 10; matrix products, arithmetic and copies ran while one was open for 0% -> 0% of each run, Pallas kernels for 13% -> 14%
where the time goes in v2:
time: 112 us; the launch traced here: 111 us
  waiting for transfers between devices  46.8 us (42%)
  Pallas kernels  33.6 us (30%)
  starting transfers between devices  28 us (25%)
  local copies, waits for them, and re-layouts  2.05 us (2%)
    pallas_call x2, Pallas kernels, pair_call(): pl.pallas_call(kernel, grid_spec=pltpu.PrefetchScalarGridSpec(num_scalar_...  25.7 us
    ppermute x15, waiting for transfers between devices, over_chan(): return lax.ppermute(a, 'chan', perm)  23.3 us
    ppermute x15, starting transfers between devices, over_chan(): return lax.ppermute(a, 'chan', perm)  15.2 us
    all_to_all x1, waiting for transfers between devices, stages(): lax.all_to_all(slots, 'win', split_axis=0, concat_axis=0, tiled=True)  13.3 us
    ppermute x7, waiting for transfers between devices, over_win(): return lax.ppermute(a, 'win', perm)  10.2 us
    ppermute x7, starting transfers between devices, over_win(): return lax.ppermute(a, 'win', perm)  7.46 us
    pallas_call x1, Pallas kernels, spectra_call(): pl.pallas_call(kernel, grid=(steps,), in_specs=[pl.BlockSpec((SPAN, windo...  5.74 us
    all_to_all x1, starting transfers between devices, stages(): lax.all_to_all(slots, 'win', split_axis=0, concat_axis=0, tiled=True)  5.44 us
  transfers between devices with their start and end apart: 23, of which 10 were waited for; matrix products, arithmetic and copies ran while one was open for 0% of the time, Pallas kernels for 14%

profile of v2, /device:TPU:0, one launch (start us, length us, event | category | flops | bytes accessed | tf_op | source)
XLA Modules:
  0.0 110.8 jit_solution(17180464850787723991)
XLA Ops:
  0.0 5.7 %spectra.1 = (bf16[129,16,128]{2,1,0:T(8,128)(2,1)}, bf16[8,17,16,128]{3,2,1,0:T(8,128)(2,1)}) custom-call(bf16[1500,8,128]{2,1,0:T(8,128)(2,1)} %bitcast.25, s32[8,128]{1,0:T(8,128)} %v_ref.1, bf16[256,1536]{1,0:T(8,128)(2,1)} %constant.230.clone.t_ref), custom_call_target="tpu_custom_call" | custom-call | tf_op jit(solution)/shard_map/spectra/pallas_call | solution.py:101
  5.7 3.1 %collective-permute-start.2 = (bf16[129,16,128]{2,1,0:T(8,128)(2,1)}, bf16[129,16,128]{2,1,0:T(8,128)(2,1)S(1)}, u32[]{:S(2)}, u32[]{:S(2)}) collective-permute-start(bf16[129,16,128]{2,1,0:T(8,128)(2,1)} %get-tuple-element.7.refs_0_), channel_id=1, source_target_pairs={{0,6},{1,7},{2,0},{3,1},{4,2},{5,3},{6,4},{7,5},{8,14},{9,15},{10,... | collective-permute-start | bytes 1585160 | tf_op jit(solution)/shard_map/ppermute | solution.py:311
  8.9 0.0 collective-permute-start.1
  8.9 5.4 %all-to-all-start = ((bf16[8,17,16,128]{3,2,1,0:T(8,128)(2,1)}), bf16[8,17,16,128]{3,2,1,0:T(8,128)(2,1)S(1)}, u32[]{:S(2)}, u32[]{:S(2)}) async-start(bf16[8,17,16,128]{3,2,1,0:T(8,128)(2,1)} %get-tuple-element.8), calls=%async_computation | async-start | bytes 1114112 | tf_op jit(solution)/shard_map/all_to_all | solution.py:321
  14.3 2.0 %collective-permute-start = (bf16[129,16,128]{2,1,0:T(8,128)(2,1)}, bf16[129,16,128]{2,1,0:T(8,128)(2,1)S(1)}, u32[]{:S(2)}, u32[]{:S(2)}) collective-permute-start(bf16[129,16,128]{2,1,0:T(8,128)(2,1)} %get-tuple-element.7.refs_0_), channel_id=1, source_target_pairs={{0,1},{1,0},{2,3},{3,2},{4,5},{5,4},{6,7},{7,6},{8,9},{9,8},{10,11... | collective-permute-start | bytes 1585160 | tf_op jit(solution)/shard_map/ppermute | solution.py:311
  16.3 0.1 stack.99.order_ref.place_ref
  16.4 13.3 %all-to-all-done.p_ref = bf16[8,17,16,128]{3,2,1,0:T(8,128)(2,1)S(1)} async-done(((bf16[8,17,16,128]{3,2,1,0:T(8,128)(2,1)}), bf16[8,17,16,128]{3,2,1,0:T(8,128)(2,1)S(1)}, u32[]{:S(2)}, u32[]{:S(2)}) %all-to-all-start) | async-done | bytes 557088 | tf_op jit(solution)/shard_map/all_to_all | solution.py:321
  29.7 2.2 %slot.1.refs_8_ = bf16[129,16,128]{2,1,0:T(8,128)(2,1)S(1)} custom-call(s32[24]{0:T(128)S(1)} %stack.99.order_ref.place_ref, bf16[8,17,16,128]{3,2,1,0:T(8,128)(2,1)S(1)} %all-to-all-done.p_ref), custom_call_target="tpu_custom_call" | custom-call | tf_op jit(solution)/shard_map/slot/pallas_call | solution.py:161
  32.0 4.1 %collective-permute-start.20 = (bf16[129,16,128]{2,1,0:T(8,128)(2,1)S(1)}, bf16[129,16,128]{2,1,0:T(8,128)(2,1)S(1)}, u32[]{:S(2)}, u32[]{:S(2)}) collective-permute-start(bf16[129,16,128]{2,1,0:T(8,128)(2,1)S(1)} %slot.1.refs_8_), channel_id=1, source_target_pairs={{0,96},{8,104},{16,112},{24,120},{32,0},{40,8},{48,16},{56,24},{64... | collective-permute-start | bytes 1585160 | tf_op jit(solution)/shard_map/ppermute | solution.py:307
  36.1 0.0 collective-permute-start.17
  36.1 0.0 collective-permute-done.2.refs_3_
  36.1 0.0 collective-permute-start.12
  36.1 0.0 collective-permute-done.1.refs_2_
  36.1 3.1 %collective-permute-start.7 = (bf16[129,16,128]{2,1,0:T(8,128)(2,1)S(1)}, bf16[129,16,128]{2,1,0:T(8,128)(2,1)S(1)}, u32[]{:S(2)}, u32[]{:S(2)}) collective-permute-start(bf16[129,16,128]{2,1,0:T(8,128)(2,1)S(1)} %slot.1.refs_8_), channel_id=1, source_target_pairs={{0,16},{8,24},{16,0},{24,8},{32,48},{40,56},{48,32},{56,40},{64,80... | collective-permute-start | bytes 1585160 | tf_op jit(solution)/shard_map/ppermute | solution.py:307
  39.2 0.0 collective-permute-done.refs_1_
  39.2 0.0 collective-permute-start.5
  39.2 6.3 %collective-permute-done.20.refs_14_ = bf16[129,16,128]{2,1,0:T(8,128)(2,1)S(1)} collective-permute-done((bf16[129,16,128]{2,1,0:T(8,128)(2,1)S(1)}, bf16[129,16,128]{2,1,0:T(8,128)(2,1)S(1)}, u32[]{:S(2)}, u32[]{:S(2)}) %collective-permute-start.20) | collective-permute-done | bytes 528416 | tf_op jit(solution)/shard_map/ppermute | solution.py:307
  45.5 1.3 %collective-permute-start.4 = (bf16[129,16,128]{2,1,0:T(8,128)(2,1)S(1)}, bf16[129,16,128]{2,1,0:T(8,128)(2,1)S(1)}, u32[]{:S(2)}, u32[]{:S(2)}) collective-permute-start(bf16[129,16,128]{2,1,0:T(8,128)(2,1)S(1)} %collective-permute-done.refs_1_), channel_id=1, source_target_pairs={{0,6},{1,7},{2,0},{3,1},{4,2},{5,3},{6,4},{7,5},{8,14},{9,15},{10,... | collective-permute-start | bytes 1585160 | tf_op jit(solution)/shard_map/ppermute | solution.py:311
  46.8 0.0 collective-permute-done.17.refs_9_
  46.8 0.7 collective-permute-start.3
  47.5 4.2 %collective-permute-done.12.refs_12_ = bf16[129,16,128]{2,1,0:T(8,128)(2,1)S(1)} collective-permute-done((bf16[129,16,128]{2,1,0:T(8,128)(2,1)S(1)}, bf16[129,16,128]{2,1,0:T(8,128)(2,1)S(1)}, u32[]{:S(2)}, u32[]{:S(2)}) %collective-permute-start.12) | collective-permute-done | bytes 528416 | tf_op jit(solution)/shard_map/ppermute | solution.py:307
  51.7 0.0 collective-permute-start.21
  51.7 0.4 collective-permute-done.7.refs_10_
  52.1 2.9 %collective-permute-start.10 = (bf16[129,16,128]{2,1,0:T(8,128)(2,1)S(1)}, bf16[129,16,128]{2,1,0:T(8,128)(2,1)S(1)}, u32[]{:S(2)}, u32[]{:S(2)}) collective-permute-start(bf16[129,16,128]{2,1,0:T(8,128)(2,1)S(1)} %collective-permute-done.7.refs_10_), channel_id=1, source_target_pairs={{0,96},{8,104},{16,112},{24,120},{32,0},{40,8},{48,16},{56,24},{64... | collective-permute-start | bytes 1585160 | tf_op jit(solution)/shard_map/ppermute | solution.py:307
  55.0 0.3 collective-permute-done.5.refs_6_
  55.3 0.0 collective-permute-start.19
  55.3 1.2 %collective-permute-done.4.refs_5_ = bf16[129,16,128]{2,1,0:T(8,128)(2,1)S(1)} collective-permute-done((bf16[129,16,128]{2,1,0:T(8,128)(2,1)S(1)}, bf16[129,16,128]{2,1,0:T(8,128)(2,1)S(1)}, u32[]{:S(2)}, u32[]{:S(2)}) %collective-permute-start.4) | collective-permute-done | bytes 528416 | tf_op jit(solution)/shard_map/ppermute | solution.py:311
  56.5 0.7 collective-permute-start.13
  57.2 8.7 %collective-permute-done.3.refs_4_ = bf16[129,16,128]{2,1,0:T(8,128)(2,1)S(1)} collective-permute-done((bf16[129,16,128]{2,1,0:T(8,128)(2,1)S(1)}, bf16[129,16,128]{2,1,0:T(8,128)(2,1)S(1)}, u32[]{:S(2)}, u32[]{:S(2)}) %collective-permute-start.3) | collective-permute-done | bytes 528416 | tf_op jit(solution)/shard_map/ppermute | solution.py:311
  65.9 0.0 collective-permute-start.18
  65.9 0.0 collective-permute-done.21.refs_15_
  65.9 0.0 collective-permute-start.8
  65.9 0.3 collective-permute-done.10.refs_10_
  66.1 3.3 %collective-permute-start.15 = (bf16[129,16,128]{2,1,0:T(8,128)(2,1)S(1)}, bf16[129,16,128]{2,1,0:T(8,128)(2,1)S(1)}, u32[]{:S(2)}, u32[]{:S(2)}) collective-permute-start(bf16[129,16,128]{2,1,0:T(8,128)(2,1)S(1)} %collective-permute-done.10.refs_10_), channel_id=1, source_target_pairs={{0,96},{8,104},{16,112},{24,120},{32,0},{40,8},{48,16},{56,24},{64... | collective-permute-start | bytes 1585160 | tf_op jit(solution)/shard_map/ppermute | solution.py:307
  69.5 0.0 collective-permute-done.19.refs_13_
  69.5 0.3 collective-permute-start.6
  69.8 2.3 %collective-permute-done.13.refs_12_ = bf16[129,16,128]{2,1,0:T(8,128)(2,1)S(1)} collective-permute-done((bf16[129,16,128]{2,1,0:T(8,128)(2,1)S(1)}, bf16[129,16,128]{2,1,0:T(8,128)(2,1)S(1)}, u32[]{:S(2)}, u32[]{:S(2)}) %collective-permute-start.13) | collective-permute-done | bytes 528416 | tf_op jit(solution)/shard_map/ppermute | solution.py:307
  72.1 0.0 collective-permute-start.11
  72.1 0.0 collective-permute-done.18.refs_11_
  72.1 0.5 collective-permute-start.14
  72.6 9.9 %collective-permute-done.8.refs_8_ = bf16[129,16,128]{2,1,0:T(8,128)(2,1)S(1)} collective-permute-done((bf16[129,16,128]{2,1,0:T(8,128)(2,1)S(1)}, bf16[129,16,128]{2,1,0:T(8,128)(2,1)S(1)}, u32[]{:S(2)}, u32[]{:S(2)}) %collective-permute-start.8) | collective-permute-done | bytes 528416 | tf_op jit(solution)/shard_map/ppermute | solution.py:307
  82.5 0.0 collective-permute-start.9
  82.5 0.0 collective-permute-done.15.refs_14_
  82.5 0.5 collective-permute-start.16
  83.0 0.0 collective-permute-done.6.refs_7_
  83.0 0.0 copy-start
  83.0 1.0 copy-done
  84.0 0.0 copy-start.1
  84.0 0.9 copy-done.1
  84.9 12.8 %shard_map.46.refs_17_ = f32[128,16,1,16,128]{4,3,2,1,0:T(8,128)} custom-call(s32[24]{0:T(128)S(1)} %stack.99.order_ref.place_ref, bf16[129,16,128]{2,1,0:T(8,128)(2,1)S(1)} %copy-done, bf16[129,16,128]{2,1,0:T(8,128)(2,1)S(1)} %collective-permute-done.refs_1_, bf16[129,16,128]{2,1,0:T(8,128)(2,1)S(1)} %collective-permute-done.1.refs_2_, ...), custom_call_target="tpu_custom_call" | custom-call | flops 4303355904 | bytes 8454144 | tf_op jit(solution)/shard_map/pallas_call | solution.py:273
  97.8 0.0 collective-permute-done.14.refs_13_
  97.8 0.0 collective-permute-done.11.refs_11_
  97.8 0.0 collective-permute-done.9.refs_9_
  97.8 0.0 collective-permute-done.16.refs_15_
  97.8 12.9 %shard_map.47 = f32[128,16,1,16,128]{4,3,2,1,0:T(8,128)} custom-call(s32[24]{0:T(128)S(1)} %stack.99.order_ref.place_ref, bf16[129,16,128]{2,1,0:T(8,128)(2,1)S(1)} %copy-done, bf16[129,16,128]{2,1,0:T(8,128)(2,1)S(1)} %collective-permute-done.refs_1_, bf16[129,16,128]{2,1,0:T(8,128)(2,1)S(1)} %collective-permute-done.1.refs_2_, ...), custom_call_target="tpu_custom_call", output_to_operand_aliasing={{}: (18, {})} | custom-call | flops 4303355904 | bytes 8454144 | tf_op jit(solution)/shard_map/pallas_call | solution.py:273
Async XLA Ops:
  5.7 30.3 %collective-permute-start.2 = (bf16[129,16,128]{2,1,0:T(8,128)(2,1)}, bf16[129,16,128]{2,1,0:T(8,128)(2,1)S(1)}, u32[]{:S(2)}, u32[]{:S(2)}) collective-permute-start(bf16[129,16,128]{2,1,0:T(8,128)(2,1)} %get-tuple-element.7.refs_0_), channel_id=1, source_target_pairs={{0,6},{1,7},{2,0},{3,1},{4,2},{5,3},{6,4},{7,5},{8,14},{9,15},{10,... | collective-permute-start | bytes 1585160 | tf_op jit(solution)/shard_map/ppermute | solution.py:311
  8.9 27.2 %collective-permute-start.1 = (bf16[129,16,128]{2,1,0:T(8,128)(2,1)}, bf16[129,16,128]{2,1,0:T(8,128)(2,1)S(1)}, u32[]{:S(2)}, u32[]{:S(2)}) collective-permute-start(bf16[129,16,128]{2,1,0:T(8,128)(2,1)} %get-tuple-element.7.refs_0_), channel_id=1, source_target_pairs={{0,2},{1,3},{2,4},{3,5},{4,6},{5,7},{6,0},{7,1},{8,10},{9,11},{10,... | collective-permute-start | bytes 1585160 | tf_op jit(solution)/shard_map/ppermute | solution.py:311
  8.9 20.9 %all-to-all-start = ((bf16[8,17,16,128]{3,2,1,0:T(8,128)(2,1)}), bf16[8,17,16,128]{3,2,1,0:T(8,128)(2,1)S(1)}, u32[]{:S(2)}, u32[]{:S(2)}) async-start(bf16[8,17,16,128]{3,2,1,0:T(8,128)(2,1)} %get-tuple-element.8), calls=%async_computation | async-start | bytes 1114112 | tf_op jit(solution)/shard_map/all_to_all | solution.py:321
  14.3 24.9 %collective-permute-start = (bf16[129,16,128]{2,1,0:T(8,128)(2,1)}, bf16[129,16,128]{2,1,0:T(8,128)(2,1)S(1)}, u32[]{:S(2)}, u32[]{:S(2)}) collective-permute-start(bf16[129,16,128]{2,1,0:T(8,128)(2,1)} %get-tuple-element.7.refs_0_), channel_id=1, source_target_pairs={{0,1},{1,0},{2,3},{3,2},{4,5},{5,4},{6,7},{7,6},{8,9},{9,8},{10,11... | collective-permute-start | bytes 1585160 | tf_op jit(solution)/shard_map/ppermute | solution.py:311
  32.0 13.5 %collective-permute-start.20 = (bf16[129,16,128]{2,1,0:T(8,128)(2,1)S(1)}, bf16[129,16,128]{2,1,0:T(8,128)(2,1)S(1)}, u32[]{:S(2)}, u32[]{:S(2)}) collective-permute-start(bf16[129,16,128]{2,1,0:T(8,128)(2,1)S(1)} %slot.1.refs_8_), channel_id=1, source_target_pairs={{0,96},{8,104},{16,112},{24,120},{32,0},{40,8},{48,16},{56,24},{64... | collective-permute-start | bytes 1585160 | tf_op jit(solution)/shard_map/ppermute | solution.py:307
  36.1 10.7 %collective-permute-start.17 = (bf16[129,16,128]{2,1,0:T(8,128)(2,1)S(1)}, bf16[129,16,128]{2,1,0:T(8,128)(2,1)S(1)}, u32[]{:S(2)}, u32[]{:S(2)}) collective-permute-start(bf16[129,16,128]{2,1,0:T(8,128)(2,1)S(1)} %slot.1.refs_8_), channel_id=1, source_target_pairs={{0,8},{8,0},{16,24},{24,16},{32,40},{40,32},{48,56},{56,48},{64,72... | collective-permute-start | bytes 1585160 | tf_op jit(solution)/shard_map/ppermute | solution.py:307
  36.1 15.6 %collective-permute-start.12 = (bf16[129,16,128]{2,1,0:T(8,128)(2,1)S(1)}, bf16[129,16,128]{2,1,0:T(8,128)(2,1)S(1)}, u32[]{:S(2)}, u32[]{:S(2)}) collective-permute-start(bf16[129,16,128]{2,1,0:T(8,128)(2,1)S(1)} %slot.1.refs_8_), channel_id=1, source_target_pairs={{0,32},{8,40},{16,48},{24,56},{32,64},{40,72},{48,80},{56,88},{64,... | collective-permute-start | bytes 1585160 | tf_op jit(solution)/shard_map/ppermute | solution.py:307
  36.1 16.0 %collective-permute-start.7 = (bf16[129,16,128]{2,1,0:T(8,128)(2,1)S(1)}, bf16[129,16,128]{2,1,0:T(8,128)(2,1)S(1)}, u32[]{:S(2)}, u32[]{:S(2)}) collective-permute-start(bf16[129,16,128]{2,1,0:T(8,128)(2,1)S(1)} %slot.1.refs_8_), channel_id=1, source_target_pairs={{0,16},{8,24},{16,0},{24,8},{32,48},{40,56},{48,32},{56,40},{64,80... | collective-permute-start | bytes 1585160 | tf_op jit(solution)/shard_map/ppermute | solution.py:307
  39.2 16.1 %collective-permute-start.5 = (bf16[129,16,128]{2,1,0:T(8,128)(2,1)S(1)}, bf16[129,16,128]{2,1,0:T(8,128)(2,1)S(1)}, u32[]{:S(2)}, u32[]{:S(2)}) collective-permute-start(bf16[129,16,128]{2,1,0:T(8,128)(2,1)S(1)} %collective-permute-done.1.refs_2_), channel_id=1, source_target_pairs={{0,2},{1,3},{2,4},{3,5},{4,6},{5,7},{6,0},{7,1},{8,10},{9,11},{10,... | collective-permute-start | bytes 1585160 | tf_op jit(solution)/shard_map/ppermute | solution.py:311
  45.5 11.0 %collective-permute-start.4 = (bf16[129,16,128]{2,1,0:T(8,128)(2,1)S(1)}, bf16[129,16,128]{2,1,0:T(8,128)(2,1)S(1)}, u32[]{:S(2)}, u32[]{:S(2)}) collective-permute-start(bf16[129,16,128]{2,1,0:T(8,128)(2,1)S(1)} %collective-permute-done.refs_1_), channel_id=1, source_target_pairs={{0,6},{1,7},{2,0},{3,1},{4,2},{5,3},{6,4},{7,5},{8,14},{9,15},{10,... | collective-permute-start | bytes 1585160 | tf_op jit(solution)/shard_map/ppermute | solution.py:311
  46.8 19.1 %collective-permute-start.3 = (bf16[129,16,128]{2,1,0:T(8,128)(2,1)S(1)}, bf16[129,16,128]{2,1,0:T(8,128)(2,1)S(1)}, u32[]{:S(2)}, u32[]{:S(2)}) collective-permute-start(bf16[129,16,128]{2,1,0:T(8,128)(2,1)S(1)} %collective-permute-done.refs_1_), channel_id=1, source_target_pairs={{0,2},{1,3},{2,4},{3,5},{4,6},{5,7},{6,0},{7,1},{8,10},{9,11},{10,... | collective-permute-start | bytes 1585160 | tf_op jit(solution)/shard_map/ppermute | solution.py:311
  51.7 14.2 %collective-permute-start.21 = (bf16[129,16,128]{2,1,0:T(8,128)(2,1)S(1)}, bf16[129,16,128]{2,1,0:T(8,128)(2,1)S(1)}, u32[]{:S(2)}, u32[]{:S(2)}) collective-permute-start(bf16[129,16,128]{2,1,0:T(8,128)(2,1)S(1)} %collective-permute-done.20.refs_14_), channel_id=1, source_target_pairs={{0,8},{8,0},{16,24},{24,16},{32,40},{40,32},{48,56},{56,48},{64,72... | collective-permute-start | bytes 1585160 | tf_op jit(solution)/shard_map/ppermute | solution.py:307
  52.1 14.0 %collective-permute-start.10 = (bf16[129,16,128]{2,1,0:T(8,128)(2,1)S(1)}, bf16[129,16,128]{2,1,0:T(8,128)(2,1)S(1)}, u32[]{:S(2)}, u32[]{:S(2)}) collective-permute-start(bf16[129,16,128]{2,1,0:T(8,128)(2,1)S(1)} %collective-permute-done.7.refs_10_), channel_id=1, source_target_pairs={{0,96},{8,104},{16,112},{24,120},{32,0},{40,8},{48,16},{56,24},{64... | collective-permute-start | bytes 1585160 | tf_op jit(solution)/shard_map/ppermute | solution.py:307
  55.3 14.2 %collective-permute-start.19 = (bf16[129,16,128]{2,1,0:T(8,128)(2,1)S(1)}, bf16[129,16,128]{2,1,0:T(8,128)(2,1)S(1)}, u32[]{:S(2)}, u32[]{:S(2)}) collective-permute-start(bf16[129,16,128]{2,1,0:T(8,128)(2,1)S(1)} %collective-permute-done.12.refs_12_), channel_id=1, source_target_pairs={{0,8},{8,0},{16,24},{24,16},{32,40},{40,32},{48,56},{56,48},{64,72... | collective-permute-start | bytes 1585160 | tf_op jit(solution)/shard_map/ppermute | solution.py:307
  56.5 15.6 %collective-permute-start.13 = (bf16[129,16,128]{2,1,0:T(8,128)(2,1)S(1)}, bf16[129,16,128]{2,1,0:T(8,128)(2,1)S(1)}, u32[]{:S(2)}, u32[]{:S(2)}) collective-permute-start(bf16[129,16,128]{2,1,0:T(8,128)(2,1)S(1)} %collective-permute-done.12.refs_12_), channel_id=1, source_target_pairs={{0,32},{8,40},{16,48},{24,56},{32,64},{40,72},{48,80},{56,88},{64,... | collective-permute-start | bytes 1585160 | tf_op jit(solution)/shard_map/ppermute | solution.py:307
  65.9 6.2 %collective-permute-start.18 = (bf16[129,16,128]{2,1,0:T(8,128)(2,1)S(1)}, bf16[129,16,128]{2,1,0:T(8,128)(2,1)S(1)}, u32[]{:S(2)}, u32[]{:S(2)}) collective-permute-start(bf16[129,16,128]{2,1,0:T(8,128)(2,1)S(1)} %collective-permute-done.7.refs_10_), channel_id=1, source_target_pairs={{0,8},{8,0},{16,24},{24,16},{32,40},{40,32},{48,56},{56,48},{64,72... | collective-permute-start | bytes 1585160 | tf_op jit(solution)/shard_map/ppermute | solution.py:307
  65.9 16.6 %collective-permute-start.8 = (bf16[129,16,128]{2,1,0:T(8,128)(2,1)S(1)}, bf16[129,16,128]{2,1,0:T(8,128)(2,1)S(1)}, u32[]{:S(2)}, u32[]{:S(2)}) collective-permute-start(bf16[129,16,128]{2,1,0:T(8,128)(2,1)S(1)} %collective-permute-done.7.refs_10_), channel_id=1, source_target_pairs={{0,32},{8,40},{16,48},{24,56},{32,64},{40,72},{48,80},{56,88},{64,... | collective-permute-start | bytes 1585160 | tf_op jit(solution)/shard_map/ppermute | solution.py:307
  66.1 16.3 %collective-permute-start.15 = (bf16[129,16,128]{2,1,0:T(8,128)(2,1)S(1)}, bf16[129,16,128]{2,1,0:T(8,128)(2,1)S(1)}, u32[]{:S(2)}, u32[]{:S(2)}) collective-permute-start(bf16[129,16,128]{2,1,0:T(8,128)(2,1)S(1)} %collective-permute-done.10.refs_10_), channel_id=1, source_target_pairs={{0,96},{8,104},{16,112},{24,120},{32,0},{40,8},{48,16},{56,24},{64... | collective-permute-start | bytes 1585160 | tf_op jit(solution)/shard_map/ppermute | solution.py:307
  69.5 13.5 %collective-permute-start.6 = (bf16[129,16,128]{2,1,0:T(8,128)(2,1)S(1)}, bf16[129,16,128]{2,1,0:T(8,128)(2,1)S(1)}, u32[]{:S(2)}, u32[]{:S(2)}) collective-permute-start(bf16[129,16,128]{2,1,0:T(8,128)(2,1)S(1)} %collective-permute-done.4.refs_5_), channel_id=1, source_target_pairs={{0,6},{1,7},{2,0},{3,1},{4,2},{5,3},{6,4},{7,5},{8,14},{9,15},{10,... | collective-permute-start | bytes 1585160 | tf_op jit(solution)/shard_map/ppermute | solution.py:311
  72.1 25.7 %collective-permute-start.11 = (bf16[129,16,128]{2,1,0:T(8,128)(2,1)S(1)}, bf16[129,16,128]{2,1,0:T(8,128)(2,1)S(1)}, u32[]{:S(2)}, u32[]{:S(2)}) collective-permute-start(bf16[129,16,128]{2,1,0:T(8,128)(2,1)S(1)} %collective-permute-done.10.refs_10_), channel_id=1, source_target_pairs={{0,8},{8,0},{16,24},{24,16},{32,40},{40,32},{48,56},{56,48},{64,72... | collective-permute-start | bytes 1585160 | tf_op jit(solution)/shard_map/ppermute | solution.py:307
  72.1 25.7 %collective-permute-start.14 = (bf16[129,16,128]{2,1,0:T(8,128)(2,1)S(1)}, bf16[129,16,128]{2,1,0:T(8,128)(2,1)S(1)}, u32[]{:S(2)}, u32[]{:S(2)}) collective-permute-start(bf16[129,16,128]{2,1,0:T(8,128)(2,1)S(1)} %collective-permute-done.13.refs_12_), channel_id=1, source_target_pairs={{0,8},{8,0},{16,24},{24,16},{32,40},{40,32},{48,56},{56,48},{64,72... | collective-permute-start | bytes 1585160 | tf_op jit(solution)/shard_map/ppermute | solution.py:307
  82.5 15.3 %collective-permute-start.9 = (bf16[129,16,128]{2,1,0:T(8,128)(2,1)S(1)}, bf16[129,16,128]{2,1,0:T(8,128)(2,1)S(1)}, u32[]{:S(2)}, u32[]{:S(2)}) collective-permute-start(bf16[129,16,128]{2,1,0:T(8,128)(2,1)S(1)} %collective-permute-done.8.refs_8_), channel_id=1, source_target_pairs={{0,8},{8,0},{16,24},{24,16},{32,40},{40,32},{48,56},{56,48},{64,72... | collective-permute-start | bytes 1585160 | tf_op jit(solution)/shard_map/ppermute | solution.py:307
  82.5 15.3 %collective-permute-start.16 = (bf16[129,16,128]{2,1,0:T(8,128)(2,1)S(1)}, bf16[129,16,128]{2,1,0:T(8,128)(2,1)S(1)}, u32[]{:S(2)}, u32[]{:S(2)}) collective-permute-start(bf16[129,16,128]{2,1,0:T(8,128)(2,1)S(1)} %collective-permute-done.15.refs_14_), channel_id=1, source_target_pairs={{0,8},{8,0},{16,24},{24,16},{32,40},{40,32},{48,56},{56,48},{64,72... | collective-permute-start | bytes 1585160 | tf_op jit(solution)/shard_map/ppermute | solution.py:307
  83.0 1.0 copy-start
  84.0 0.9 copy-start.1
